TPU v7x, 32 devices: a whole 2x2x4 slice. The times are simulated.
32 devices in a mesh: gx: 4 (over z), gy: 2 (over y), gz: 4 (over x, core).
Axes of the slice: x: 2, y: 2, z: 4, core: 2. Of those that a mesh axis runs over, the one named last changes fastest.
Arguments:
- density: float32 [32, 16, 512], P('gx', 'gy', 'gz'), may hold values from 0.5 to 2
- base_velocity: float32 [3, 32, 16, 512], P(None, 'gx', 'gy', 'gz'), may hold values from -0.4 to 0.4
- cells: int32 [3, 8192], P(None, ('gx', 'gy', 'gz')), may hold values from 0 to 511, as said below
- offsets: float32 [3, 8192], P(None, ('gx', 'gy', 'gz')), may hold values from 0 to 1
- target: float32 [3, 8192], P(None, ('gx', 'gy', 'gz')), may hold values from -0.4 to 0.4
- stiffness: float32 [8192], P(('gx', 'gy', 'gz')), may hold values from 0.01 to 0.1
- counts: int32 [32], P(('gx', 'gy', 'gz')), may hold values from 1 to 256, as said below
Outputs:
- forces: float32 [3, 8192], P(None, ('gx', 'gy', 'gz'))
Inputs may be any that keep to these rules, and one draw needn't show every extreme that they name: `cells`: each marker's cell lies inside the lattice block of the device that holds its slot. `counts`: some device holds exactly 256 live markers in every draw.
All inputs are finite; a program needn't handle non-finite values.
Results may differ from a plain program's by a relative error of at most 0.0001.
Values sent between devices are 32-bit elements; how exact they have to be, the bound alone decides.
A program may use at most 64 MiB of HBM per device.

v0:
```python
import jax
import jax.numpy as jnp
from jax import lax
from jax.sharding import PartitionSpec as P

ITERS = 3


def extended(cells, sides, width):
    for axis, dim in sides:
        count = lax.axis_size(axis)
        head = lax.slice_in_dim(cells, 0, width, axis=dim)
        tail = lax.slice_in_dim(cells, cells.shape[dim] - width, cells.shape[dim], axis=dim)
        cells = jnp.concatenate(
            [
                lax.ppermute(tail, axis, [(i, (i + 1) % count) for i in range(count)]),
                cells,
                lax.ppermute(head, axis, [((i + 1) % count, i) for i in range(count)]),
            ],
            axis=dim,
        )
    return cells


def moving_directions():
    listing = []
    for along_x in (-1, 0, 1):
        for along_y in (-1, 0, 1):
            for along_z in (-1, 0, 1):
                order = abs(along_x) + abs(along_y) + abs(along_z)
                if order == 1:
                    listing.append((along_x, along_y, along_z, 1.0 / 18.0))
                elif order == 2:
                    listing.append((along_x, along_y, along_z, 1.0 / 36.0))
    return listing


def delta_weights(fraction):

    def inner(radius):
        return (3.0 - 2.0 * radius + jnp.sqrt(1.0 + 4.0 * radius - 4.0 * radius * radius)) / 8.0

    def outer(radius):
        return (5.0 - 2.0 * radius - jnp.sqrt(-7.0 + 12.0 * radius - 4.0 * radius * radius)) / 8.0

    return jnp.stack(
        [outer(1.0 + fraction), inner(fraction), inner(1.0 - fraction), outer(2.0 - fraction)]
    )


def fold_axis(array, axis):
    length = array.shape[axis] - 8
    middle = lax.slice_in_dim(array, 4, length + 4, axis=axis)
    lower = lax.slice_in_dim(array, 0, 2, axis=axis)
    upper = lax.slice_in_dim(array, length + 6, length + 8, axis=axis)
    low_padding = [(0, 0)] * array.ndim
    low_padding[axis] = (0, length - 2)
    high_padding = [(0, 0)] * array.ndim
    high_padding[axis] = (length - 2, 0)
    return middle + jnp.pad(lower, low_padding) + jnp.pad(upper, high_padding)


def fold_ghosts(summed):
    return fold_axis(fold_axis(fold_axis(summed, 1), 2), 3)


def axis_rows(local, fraction, offset, extent):
    places = local[None, :] + jnp.arange(4, dtype=jnp.int32)[:, None] + offset
    hits = (places[:, :, None] == jnp.arange(extent, dtype=jnp.int32)[None, None, :]).astype(
        jnp.float32
    )
    return jnp.sum(delta_weights(fraction)[:, :, None] * hits, axis=0)


def make_tables(local, fractions, offset, extents):
    table_x = axis_rows(local[0], fractions[0], offset, extents[0]).T
    table_y = axis_rows(local[1], fractions[1], offset, extents[1]).T
    table_z = axis_rows(local[2], fractions[2], offset, extents[2])
    return (table_x, table_y, table_z)


def spread_dense(vector, tables):
    table_x, table_y, table_z = tables
    weighted = vector[:, None, None, :] * table_x[None, :, None, :] * table_y[None, None, :, :]
    return jnp.einsum("cxym,mz->cxyz", weighted, table_z, precision=lax.Precision.HIGHEST)


def interpolate_dense(field, tables):
    table_x, table_y, table_z = tables
    partial_rows = jnp.einsum("cxyz,mz->cxym", field, table_z, precision=lax.Precision.HIGHEST)
    return jnp.sum(partial_rows * (table_x[:, None, :] * table_y[None, :, :])[None], axis=(1, 2))


def body(density, base_velocity, cells, offsets, target, stiffness, counts):
    size_x, size_y, size_z = density.shape
    capacity = cells.shape[1]
    anchor = jnp.stack(
        [
            lax.axis_index("gx") * size_x,
            lax.axis_index("gy") * size_y,
            lax.axis_index("gz") * size_z,
        ]
    )
    own_tables = make_tables(
        cells - anchor[:, None], offsets, 1, (size_x + 4, size_y + 4, size_z + 4)
    )
    live = (jnp.arange(capacity, dtype=jnp.int32) < counts[0]).astype(jnp.float32)
    scale = lax.rsqrt(density)
    stacked = jnp.concatenate([base_velocity, scale[None]], axis=0)
    fields = extended(stacked, (("gx", 1), ("gy", 2), ("gz", 3)), 3)
    base_wide = fields[:3, 1 : size_x + 5, 1 : size_y + 5, 1 : size_z + 5]
    directions = moving_directions()

    def apply(vector):
        summed = extended(spread_dense(vector, own_tables), (("gx", 1), ("gy", 2), ("gz", 3)), 2)
        moved = scale * fold_ghosts(summed)
        populations = jnp.stack(
            [
                3.0 * share * (along_x * moved[0] + along_y * moved[1] + along_z * moved[2])
                for along_x, along_y, along_z, share in directions
            ]
        )
        wide = extended(populations, (("gx", 1), ("gy", 2), ("gz", 3)), 1)
        post = jnp.zeros((3, size_x, size_y, size_z), jnp.float32)
        for number, (along_x, along_y, along_z, share) in enumerate(directions):
            shifted = wide[
                number,
                1 - along_x : 1 - along_x + size_x,
                1 - along_y : 1 - along_y + size_y,
                1 - along_z : 1 - along_z + size_z,
            ]
            post = post + jnp.stack([along_x * shifted, along_y * shifted, along_z * shifted])
        velocity = scale * (moved + post) * 0.5
        velocity_wide = extended(velocity, (("gx", 1), ("gy", 2), ("gz", 3)), 2)
        return live * (interpolate_dense(velocity_wide, own_tables) + stiffness * vector)

    def both_products(vector, image):
        return lax.psum((jnp.sum(vector * vector), jnp.sum(vector * image)), ("gx", "gy", "gz"))

    right = live * (target - interpolate_dense(base_wide, own_tables))
    solution = jnp.zeros_like(right)
    residual = right
    image = apply(residual)
    norm_now, product = both_products(residual, image)
    alpha = norm_now / product
    direction = residual
    along = image
    for step in range(ITERS):
        solution = solution + alpha * direction
        residual = residual - alpha * along
        if step + 1 < ITERS:
            image = apply(residual)
            norm_next, product = both_products(residual, image)
            ratio = norm_next / norm_now
            alpha = norm_next / (product - ratio * norm_next / alpha)
            direction = residual + ratio * direction
            along = image + ratio * along
            norm_now = norm_next
    return solution


def solution(mesh):
    return jax.shard_map(
        body,
        mesh=mesh,
        in_specs=(
            P("gx", "gy", "gz"),
            P(None, "gx", "gy", "gz"),
            P(None, ("gx", "gy", "gz")),
            P(None, ("gx", "gy", "gz")),
            P(None, ("gx", "gy", "gz")),
            P(("gx", "gy", "gz")),
            P(("gx", "gy", "gz")),
        ),
        out_specs=P(None, ("gx", "gy", "gz")),
        check_vma=False,
    )
```

profile of v0, /device:TPU:0, one launch (start us, length us, event | category | flops | bytes accessed | tf_op | source)
XLA Modules:
  0.0 385.7 jit_solution(5179906545613144514)
XLA Ops:
  1.6 3.1 collective-permute-start
  4.7 2.1 collective-permute-start.1
  12.8 3.4 collective-permute-done.2
  19.6 9.3 %collective-permute-done.4 = f32[4,14,14,3]{3,2,1,0:T(8,128)S(1)} collective-permute-done((f32[4,14,14,3]{3,2,1,0:T(8,128)S(1)}, f32[4,14,14,3]{3,2,1,0:T(8,128)S(1)}, u32[]{:S(2)}, u32[]{:S(2)}) %collective-permute-start.4) | collective-permute-done | bytes 9440 | tf_op jit(solution)/shard_map/ppermute | solution.py:16
  31.6 3.6 collective-permute-start.7
  35.2 3.7 collective-permute-done.6
  41.3 3.6 collective-permute-done.8
  48.2 8.3 %collective-permute-done.10 = f32[3,16,16,2]{3,2,1,0:T(8,128)S(1)} collective-permute-done((f32[3,16,16,2]{3,2,1,0:T(8,128)S(1)}, f32[3,16,16,2]{3,2,1,0:T(8,128)S(1)}, u32[]{:S(2)}, u32[]{:S(2)}) %collective-permute-start.10) | collective-permute-done | bytes 6176 | tf_op jit(solution)/shard_map/ppermute | solution.py:16
  58.3 2.0 collective-permute-start.12
  60.2 1.9 collective-permute-start.13
  62.1 3.0 collective-permute-done.12
  68.9 3.4 collective-permute-done.14
  75.1 2.1 copy.20
  81.7 2.4 copy.23
  87.0 2.8 collective-permute-start.19
  93.7 2.1 collective-permute-done.20
  98.9 5.8 %collective-permute-done.22 = f32[3,12,12,2]{3,2,1,0:T(8,128)S(1)} collective-permute-done((f32[3,12,12,2]{3,2,1,0:T(8,128)S(1)}, f32[3,12,12,2]{3,2,1,0:T(8,128)S(1)}, u32[]{:S(2)}, u32[]{:S(2)}) %collective-permute-start.22) | collective-permute-done | bytes 3488 | tf_op jit(solution)/shard_map/ppermute | solution.py:16
  107.0 39.5 %all-reduce.11 = (f32[]{:T(128)}, f32[]{:T(128)}) all-reduce(f32[]{:T(128)} %get-tuple-element.10, f32[]{:T(128)} %get-tuple-element.9), channel_id=1, replica_groups=mesh['gx'=4,'gy'=2,'gz'=4] {'gx','gy','gz'}, use_global_device_ids=true, to_apply=%region_5.6 | all-reduce | flops 2 | bytes 16 | tf_op jit(solution)/shard_map/psum | solution.py:138
  148.5 2.2 collective-permute-start.24
  152.4 3.1 collective-permute-done.24
  156.5 2.2 collective-permute-start.26
  158.8 2.8 collective-permute-done.26
  165.5 8.3 %collective-permute-done.28 = f32[3,16,16,2]{3,2,1,0:T(8,128)S(1)} collective-permute-done((f32[3,16,16,2]{3,2,1,0:T(8,128)S(1)}, f32[3,16,16,2]{3,2,1,0:T(8,128)S(1)}, u32[]{:S(2)}, u32[]{:S(2)}) %collective-permute-start.28) | collective-permute-done | bytes 6176 | tf_op jit(solution)/shard_map/ppermute | solution.py:16
  176.2 3.1 collective-permute-start.31
  179.4 3.0 collective-permute-done.30
  185.1 3.5 collective-permute-done.32
  191.5 2.1 copy.24
  198.1 2.4 copy.27
  203.8 2.4 collective-permute-start.37
  206.2 2.1 collective-permute-done.36
  210.4 2.1 collective-permute-done.38
  215.4 6.2 %collective-permute-done.40 = f32[3,12,12,2]{3,2,1,0:T(8,128)S(1)} collective-permute-done((f32[3,12,12,2]{3,2,1,0:T(8,128)S(1)}, f32[3,12,12,2]{3,2,1,0:T(8,128)S(1)}, u32[]{:S(2)}, u32[]{:S(2)}) %collective-permute-start.40) | collective-permute-done | bytes 3488 | tf_op jit(solution)/shard_map/ppermute | solution.py:16
  223.2 39.6 %all-reduce.10 = (f32[]{:T(128)}, f32[]{:T(128)}) all-reduce(f32[]{:T(128)} %get-tuple-element.8, f32[]{:T(128)} %get-tuple-element.7), channel_id=1, replica_groups=mesh['gx'=4,'gy'=2,'gz'=4] {'gx','gy','gz'}, use_global_device_ids=true, to_apply=%region_10.11 | all-reduce | flops 2 | bytes 16 | tf_op jit(solution)/shard_map/psum | solution.py:138
  267.6 2.2 collective-permute-start.42
  271.5 3.0 collective-permute-done.42
  275.5 2.2 collective-permute-start.44
  277.8 2.8 collective-permute-done.44
  284.5 8.4 %collective-permute-done.46 = f32[3,16,16,2]{3,2,1,0:T(8,128)S(1)} collective-permute-done((f32[3,16,16,2]{3,2,1,0:T(8,128)S(1)}, f32[3,16,16,2]{3,2,1,0:T(8,128)S(1)}, u32[]{:S(2)}, u32[]{:S(2)}) %collective-permute-start.46) | collective-permute-done | bytes 6176 | tf_op jit(solution)/shard_map/ppermute | solution.py:16
  295.4 3.1 collective-permute-start.49
  298.5 3.1 collective-permute-done.48
  304.2 3.5 collective-permute-done.50
  310.6 2.1 copy.28
  317.1 2.4 copy.31
  322.7 2.5 collective-permute-start.55
  325.2 1.8 collective-permute-done.54
  329.2 2.2 collective-permute-done.56
  334.2 6.1 %collective-permute-done.58 = f32[3,12,12,2]{3,2,1,0:T(8,128)S(1)} collective-permute-done((f32[3,12,12,2]{3,2,1,0:T(8,128)S(1)}, f32[3,12,12,2]{3,2,1,0:T(8,128)S(1)}, u32[]{:S(2)}, u32[]{:S(2)}) %collective-permute-start.58) | collective-permute-done | bytes 3488 | tf_op jit(solution)/shard_map/ppermute | solution.py:16
  342.0 39.6 %all-reduce.9 = (f32[]{:T(128)}, f32[]{:T(128)}) all-reduce(f32[]{:T(128)} %get-tuple-element.6, f32[]{:T(128)} %get-tuple-element.5), channel_id=1, replica_groups=mesh['gx'=4,'gy'=2,'gz'=4] {'gx','gy','gz'}, use_global_device_ids=true, to_apply=%region_15.16 | all-reduce | flops 2 | bytes 16 | tf_op jit(solution)/shard_map/psum | solution.py:138
  (322 shorter events, 102.9 us)
Async XLA Ops:
  1.6 7.7 %collective-permute-start = (f32[4,3,8,128]{3,2,1,0:T(8,128)S(1)}, f32[4,3,8,128]{3,2,1,0:T(8,128)S(1)}, u32[]{:S(2)}, u32[]{:S(2)}) collective-permute-start(f32[4,3,8,128]{3,2,1,0:T(8,128)S(1)} %get-tuple-element.291), channel_id=1, source_target_pairs={{0,8},{8,16},{16,24},{24,0},{1,9},{9,17},{17,25},{25,1},{2,10},{10... | collective-permute-start | bytes 147464 | tf_op jit(solution)/shard_map/ppermute | solution.py:16
  4.7 4.6 %collective-permute-start.1 = (f32[4,3,8,128]{3,2,1,0:T(8,128)S(1)}, f32[4,3,8,128]{3,2,1,0:T(8,128)S(1)}, u32[]{:S(2)}, u32[]{:S(2)}) collective-permute-start(f32[4,3,8,128]{3,2,1,0:T(8,128)S(1)} %get-tuple-element.292), channel_id=1, source_target_pairs={{8,0},{16,8},{24,16},{0,24},{9,1},{17,9},{25,17},{1,25},{10,2},{18... | collective-permute-start | bytes 147464 | tf_op jit(solution)/shard_map/ppermute | solution.py:18
  10.3 5.9 %collective-permute-start.2 = (f32[4,14,3,128]{3,2,1,0:T(4,128)S(1)}, f32[4,14,3,128]{3,2,1,0:T(4,128)S(1)}, u32[]{:S(2)}, u32[]{:S(2)}) collective-permute-start(f32[4,14,3,128]{3,2,1,0:T(4,128)S(1)} %get-tuple-element.283), channel_id=1, source_target_pairs={{0,4},{4,0},{1,5},{5,1},{2,6},{6,2},{3,7},{7,3},{8,12},{12,8},{9,1... | collective-permute-start | bytes 258056 | tf_op jit(solution)/shard_map/ppermute | solution.py:16
  12.1 5.4 %collective-permute-start.3 = (f32[4,14,3,128]{3,2,1,0:T(4,128)S(1)}, f32[4,14,3,128]{3,2,1,0:T(4,128)S(1)}, u32[]{:S(2)}, u32[]{:S(2)}) collective-permute-start(f32[4,14,3,128]{3,2,1,0:T(4,128)S(1)} %get-tuple-element.284), channel_id=1, source_target_pairs={{4,0},{0,4},{5,1},{1,5},{6,2},{2,6},{7,3},{3,7},{12,8},{8,12},{13,... | collective-permute-start | bytes 258056 | tf_op jit(solution)/shard_map/ppermute | solution.py:18
  17.8 11.1 %collective-permute-start.4 = (f32[4,14,14,3]{3,2,1,0:T(8,128)S(1)}, f32[4,14,14,3]{3,2,1,0:T(8,128)S(1)}, u32[]{:S(2)}, u32[]{:S(2)}) collective-permute-start(f32[4,14,14,3]{3,2,1,0:T(8,128)S(1)} %get-tuple-element.275), channel_id=1, source_target_pairs={{0,1},{1,2},{2,3},{3,0},{4,5},{5,6},{6,7},{7,4},{8,9},{9,10},{10,1... | collective-permute-start | bytes 28232 | tf_op jit(solution)/shard_map/ppermute | solution.py:16
  17.8 11.8 %collective-permute-start.5 = (f32[4,14,14,3]{3,2,1,0:T(8,128)S(1)}, f32[4,14,14,3]{3,2,1,0:T(8,128)S(1)}, u32[]{:S(2)}, u32[]{:S(2)}) collective-permute-start(f32[4,14,14,3]{3,2,1,0:T(8,128)S(1)} %get-tuple-element.276), channel_id=1, source_target_pairs={{1,0},{2,1},{3,2},{0,3},{5,4},{6,5},{7,6},{4,7},{9,8},{10,9},{11,1... | collective-permute-start | bytes 28232 | tf_op jit(solution)/shard_map/ppermute | solution.py:18
  31.3 7.6 %collective-permute-start.6 = (f32[3,2,12,132]{3,2,1,0:T(8,128)S(1)}, f32[3,2,12,132]{3,2,1,0:T(8,128)S(1)}, u32[]{:S(2)}, u32[]{:S(2)}) collective-permute-start(f32[3,2,12,132]{3,2,1,0:T(8,128)S(1)} %get-tuple-element.273), channel_id=1, source_target_pairs={{0,8},{8,16},{16,24},{24,0},{1,9},{9,17},{17,25},{25,1},{2,10},{10... | collective-permute-start | bytes 114056 | tf_op jit(solution)/shard_map/ppermute | solution.py:16
  31.6 7.5 %collective-permute-start.7 = (f32[3,2,12,132]{3,2,1,0:T(8,128)S(1)}, f32[3,2,12,132]{3,2,1,0:T(8,128)S(1)}, u32[]{:S(2)}, u32[]{:S(2)}) collective-permute-start(f32[3,2,12,132]{3,2,1,0:T(8,128)S(1)} %get-tuple-element.274), channel_id=1, source_target_pairs={{8,0},{16,8},{24,16},{0,24},{9,1},{17,9},{25,17},{1,25},{10,2},{18... | collective-permute-start | bytes 114056 | tf_op jit(solution)/shard_map/ppermute | solution.py:18
  39.2 5.7 %collective-permute-start.8 = (f32[3,16,2,132]{3,2,1,0:T(2,128)S(1)}, f32[3,16,2,132]{3,2,1,0:T(2,128)S(1)}, u32[]{:S(2)}, u32[]{:S(2)}) collective-permute-start(f32[3,16,2,132]{3,2,1,0:T(2,128)S(1)} %get-tuple-element.213), channel_id=1, source_target_pairs={{0,4},{4,0},{1,5},{5,1},{2,6},{6,2},{3,7},{7,3},{8,12},{12,8},{9,1... | collective-permute-start | bytes 152072 | tf_op jit(solution)/shard_map/ppermute | solution.py:16
  40.7 5.3 %collective-permute-start.9 = (f32[3,16,2,132]{3,2,1,0:T(2,128)S(1)}, f32[3,16,2,132]{3,2,1,0:T(2,128)S(1)}, u32[]{:S(2)}, u32[]{:S(2)}) collective-permute-start(f32[3,16,2,132]{3,2,1,0:T(2,128)S(1)} %get-tuple-element.214), channel_id=1, source_target_pairs={{4,0},{0,4},{5,1},{1,5},{6,2},{2,6},{7,3},{3,7},{12,8},{8,12},{13,... | collective-permute-start | bytes 152072 | tf_op jit(solution)/shard_map/ppermute | solution.py:18
  46.4 10.1 %collective-permute-start.10 = (f32[3,16,16,2]{3,2,1,0:T(8,128)S(1)}, f32[3,16,16,2]{3,2,1,0:T(8,128)S(1)}, u32[]{:S(2)}, u32[]{:S(2)}) collective-permute-start(f32[3,16,16,2]{3,2,1,0:T(8,128)S(1)} %get-tuple-element.211), channel_id=1, source_target_pairs={{0,1},{1,2},{2,3},{3,0},{4,5},{5,6},{6,7},{7,4},{8,9},{9,10},{10,1... | collective-permute-start | bytes 18440 | tf_op jit(solution)/shard_map/ppermute | solution.py:16
  46.5 10.0 %collective-permute-start.11 = (f32[3,16,16,2]{3,2,1,0:T(8,128)S(1)}, f32[3,16,16,2]{3,2,1,0:T(8,128)S(1)}, u32[]{:S(2)}, u32[]{:S(2)}) collective-permute-start(f32[3,16,16,2]{3,2,1,0:T(8,128)S(1)} %get-tuple-element.212), channel_id=1, source_target_pairs={{1,0},{2,1},{3,2},{0,3},{5,4},{6,5},{7,6},{4,7},{9,8},{10,9},{11,1... | collective-permute-start | bytes 18440 | tf_op jit(solution)/shard_map/ppermute | solution.py:18
  58.3 6.9 %collective-permute-start.12 = (f32[18,1,8,128]{3,2,1,0:T(8,128)S(1)}, f32[18,1,8,128]{3,2,1,0:T(8,128)S(1)}, u32[]{:S(2)}, u32[]{:S(2)}) collective-permute-start(f32[18,1,8,128]{3,2,1,0:T(8,128)S(1)} %get-tuple-element.271), channel_id=1, source_target_pairs={{0,8},{8,16},{16,24},{24,0},{1,9},{9,17},{17,25},{25,1},{2,10},{10... | collective-permute-start | bytes 221192 | tf_op jit(solution)/shard_map/ppermute | solution.py:16
  60.2 6.4 %collective-permute-start.13 = (f32[18,1,8,128]{3,2,1,0:T(8,128)S(1)}, f32[18,1,8,128]{3,2,1,0:T(8,128)S(1)}, u32[]{:S(2)}, u32[]{:S(2)}) collective-permute-start(f32[18,1,8,128]{3,2,1,0:T(8,128)S(1)} %get-tuple-element.272), channel_id=1, source_target_pairs={{8,0},{16,8},{24,16},{0,24},{9,1},{17,9},{25,17},{1,25},{10,2},{18... | collective-permute-start | bytes 221192 | tf_op jit(solution)/shard_map/ppermute | solution.py:18
  66.8 5.4 %collective-permute-start.14 = (f32[18,10,1,128]{3,2,1,0:T(1,128)S(1)}, f32[18,10,1,128]{3,2,1,0:T(1,128)S(1)}, u32[]{:S(2)}, u32[]{:S(2)}) collective-permute-start(f32[18,10,1,128]{3,2,1,0:T(1,128)S(1)} %get-tuple-element.231), channel_id=1, source_target_pairs={{4,0},{0,4},{5,1},{1,5},{6,2},{2,6},{7,3},{3,7},{12,8},{8,12},{13,... | collective-permute-start | bytes 276488 | tf_op jit(solution)/shard_map/ppermute | solution.py:18
  68.1 5.1 %collective-permute-start.15 = (f32[18,10,1,128]{3,2,1,0:T(1,128)S(1)}, f32[18,10,1,128]{3,2,1,0:T(1,128)S(1)}, u32[]{:S(2)}, u32[]{:S(2)}) collective-permute-start(f32[18,10,1,128]{3,2,1,0:T(1,128)S(1)} %get-tuple-element.232), channel_id=1, source_target_pairs={{0,4},{4,0},{1,5},{5,1},{2,6},{6,2},{3,7},{7,3},{8,12},{12,8},{9,1... | collective-permute-start | bytes 276488 | tf_op jit(solution)/shard_map/ppermute | solution.py:16
  85.9 5.7 %collective-permute-start.18 = (f32[3,2,8,128]{3,2,1,0:T(8,128)S(1)}, f32[3,2,8,128]{3,2,1,0:T(8,128)S(1)}, u32[]{:S(2)}, u32[]{:S(2)}) collective-permute-start(f32[3,2,8,128]{3,2,1,0:T(8,128)S(1)} %get-tuple-element.297), channel_id=1, source_target_pairs={{0,8},{8,16},{16,24},{24,0},{1,9},{9,17},{17,25},{25,1},{2,10},{10... | collective-permute-start | bytes 73736 | tf_op jit(solution)/shard_map/ppermute | solution.py:16
  87.0 4.6 %collective-permute-start.19 = (f32[3,2,8,128]{3,2,1,0:T(8,128)S(1)}, f32[3,2,8,128]{3,2,1,0:T(8,128)S(1)}, u32[]{:S(2)}, u32[]{:S(2)}) collective-permute-start(f32[3,2,8,128]{3,2,1,0:T(8,128)S(1)} %get-tuple-element.298), channel_id=1, source_target_pairs={{8,0},{16,8},{24,16},{0,24},{9,1},{17,9},{25,17},{1,25},{10,2},{18... | collective-permute-start | bytes 73736 | tf_op jit(solution)/shard_map/ppermute | solution.py:18
  97.1 7.6 %collective-permute-start.22 = (f32[3,12,12,2]{3,2,1,0:T(8,128)S(1)}, f32[3,12,12,2]{3,2,1,0:T(8,128)S(1)}, u32[]{:S(2)}, u32[]{:S(2)}) collective-permute-start(f32[3,12,12,2]{3,2,1,0:T(8,128)S(1)} %get-tuple-element.281), channel_id=1, source_target_pairs={{0,1},{1,2},{2,3},{3,0},{4,5},{5,6},{6,7},{7,4},{8,9},{9,10},{10,1... | collective-permute-start | bytes 10376 | tf_op jit(solution)/shard_map/ppermute | solution.py:16
  97.2 8.3 %collective-permute-start.23 = (f32[3,12,12,2]{3,2,1,0:T(8,128)S(1)}, f32[3,12,12,2]{3,2,1,0:T(8,128)S(1)}, u32[]{:S(2)}, u32[]{:S(2)}) collective-permute-start(f32[3,12,12,2]{3,2,1,0:T(8,128)S(1)} %get-tuple-element.282), channel_id=1, source_target_pairs={{1,0},{2,1},{3,2},{0,3},{5,4},{6,5},{7,6},{4,7},{9,8},{10,9},{11,1... | collective-permute-start | bytes 10376 | tf_op jit(solution)/shard_map/ppermute | solution.py:18
  148.5 6.9 %collective-permute-start.24 = (f32[3,2,12,132]{3,2,1,0:T(8,128)S(1)}, f32[3,2,12,132]{3,2,1,0:T(8,128)S(1)}, u32[]{:S(2)}, u32[]{:S(2)}) collective-permute-start(f32[3,2,12,132]{3,2,1,0:T(8,128)S(1)} %get-tuple-element.269), channel_id=1, source_target_pairs={{0,8},{8,16},{16,24},{24,0},{1,9},{9,17},{17,25},{25,1},{2,10},{10... | collective-permute-start | bytes 114056 | tf_op jit(solution)/shard_map/ppermute | solution.py:16
  150.7 5.7 %collective-permute-start.25 = (f32[3,2,12,132]{3,2,1,0:T(8,128)S(1)}, f32[3,2,12,132]{3,2,1,0:T(8,128)S(1)}, u32[]{:S(2)}, u32[]{:S(2)}) collective-permute-start(f32[3,2,12,132]{3,2,1,0:T(8,128)S(1)} %get-tuple-element.270), channel_id=1, source_target_pairs={{8,0},{16,8},{24,16},{0,24},{9,1},{17,9},{25,17},{1,25},{10,2},{18... | collective-permute-start | bytes 114056 | tf_op jit(solution)/shard_map/ppermute | solution.py:18
  156.5 5.1 %collective-permute-start.26 = (f32[3,16,2,132]{3,2,1,0:T(2,128)S(1)}, f32[3,16,2,132]{3,2,1,0:T(2,128)S(1)}, u32[]{:S(2)}, u32[]{:S(2)}) collective-permute-start(f32[3,16,2,132]{3,2,1,0:T(2,128)S(1)} %get-tuple-element.209), channel_id=1, source_target_pairs={{0,4},{4,0},{1,5},{5,1},{2,6},{6,2},{3,7},{7,3},{8,12},{12,8},{9,1... | collective-permute-start | bytes 152072 | tf_op jit(solution)/shard_map/ppermute | solution.py:16
  158.7 4.6 %collective-permute-start.27 = (f32[3,16,2,132]{3,2,1,0:T(2,128)S(1)}, f32[3,16,2,132]{3,2,1,0:T(2,128)S(1)}, u32[]{:S(2)}, u32[]{:S(2)}) collective-permute-start(f32[3,16,2,132]{3,2,1,0:T(2,128)S(1)} %get-tuple-element.210), channel_id=1, source_target_pairs={{4,0},{0,4},{5,1},{1,5},{6,2},{2,6},{7,3},{3,7},{12,8},{8,12},{13,... | collective-permute-start | bytes 152072 | tf_op jit(solution)/shard_map/ppermute | solution.py:18
  163.7 10.1 %collective-permute-start.28 = (f32[3,16,16,2]{3,2,1,0:T(8,128)S(1)}, f32[3,16,16,2]{3,2,1,0:T(8,128)S(1)}, u32[]{:S(2)}, u32[]{:S(2)}) collective-permute-start(f32[3,16,16,2]{3,2,1,0:T(8,128)S(1)} %get-tuple-element.207), channel_id=1, source_target_pairs={{0,1},{1,2},{2,3},{3,0},{4,5},{5,6},{6,7},{7,4},{8,9},{9,10},{10,1... | collective-permute-start | bytes 18440 | tf_op jit(solution)/shard_map/ppermute | solution.py:16
  163.7 10.0 %collective-permute-start.29 = (f32[3,16,16,2]{3,2,1,0:T(8,128)S(1)}, f32[3,16,16,2]{3,2,1,0:T(8,128)S(1)}, u32[]{:S(2)}, u32[]{:S(2)}) collective-permute-start(f32[3,16,16,2]{3,2,1,0:T(8,128)S(1)} %get-tuple-element.208), channel_id=1, source_target_pairs={{1,0},{2,1},{3,2},{0,3},{5,4},{6,5},{7,6},{4,7},{9,8},{10,9},{11,1... | collective-permute-start | bytes 18440 | tf_op jit(solution)/shard_map/ppermute | solution.py:18
  175.5 6.9 %collective-permute-start.30 = (f32[18,1,8,128]{3,2,1,0:T(8,128)S(1)}, f32[18,1,8,128]{3,2,1,0:T(8,128)S(1)}, u32[]{:S(2)}, u32[]{:S(2)}) collective-permute-start(f32[18,1,8,128]{3,2,1,0:T(8,128)S(1)} %get-tuple-element.267), channel_id=1, source_target_pairs={{0,8},{8,16},{16,24},{24,0},{1,9},{9,17},{17,25},{25,1},{2,10},{10... | collective-permute-start | bytes 221192 | tf_op jit(solution)/shard_map/ppermute | solution.py:16
  176.2 6.6 %collective-permute-start.31 = (f32[18,1,8,128]{3,2,1,0:T(8,128)S(1)}, f32[18,1,8,128]{3,2,1,0:T(8,128)S(1)}, u32[]{:S(2)}, u32[]{:S(2)}) collective-permute-start(f32[18,1,8,128]{3,2,1,0:T(8,128)S(1)} %get-tuple-element.268), channel_id=1, source_target_pairs={{8,0},{16,8},{24,16},{0,24},{9,1},{17,9},{25,17},{1,25},{10,2},{18... | collective-permute-start | bytes 221192 | tf_op jit(solution)/shard_map/ppermute | solution.py:18
  183.0 5.6 %collective-permute-start.32 = (f32[18,10,1,128]{3,2,1,0:T(1,128)S(1)}, f32[18,10,1,128]{3,2,1,0:T(1,128)S(1)}, u32[]{:S(2)}, u32[]{:S(2)}) collective-permute-start(f32[18,10,1,128]{3,2,1,0:T(1,128)S(1)} %get-tuple-element.225), channel_id=1, source_target_pairs={{4,0},{0,4},{5,1},{1,5},{6,2},{2,6},{7,3},{3,7},{12,8},{8,12},{13,... | collective-permute-start | bytes 276488 | tf_op jit(solution)/shard_map/ppermute | solution.py:18
  184.1 5.5 %collective-permute-start.33 = (f32[18,10,1,128]{3,2,1,0:T(1,128)S(1)}, f32[18,10,1,128]{3,2,1,0:T(1,128)S(1)}, u32[]{:S(2)}, u32[]{:S(2)}) collective-permute-start(f32[18,10,1,128]{3,2,1,0:T(1,128)S(1)} %get-tuple-element.226), channel_id=1, source_target_pairs={{0,4},{4,0},{1,5},{5,1},{2,6},{6,2},{3,7},{7,3},{8,12},{12,8},{9,1... | collective-permute-start | bytes 276488 | tf_op jit(solution)/shard_map/ppermute | solution.py:16
  202.3 6.0 %collective-permute-start.36 = (f32[3,2,8,128]{3,2,1,0:T(8,128)S(1)}, f32[3,2,8,128]{3,2,1,0:T(8,128)S(1)}, u32[]{:S(2)}, u32[]{:S(2)}) collective-permute-start(f32[3,2,8,128]{3,2,1,0:T(8,128)S(1)} %get-tuple-element.295), channel_id=1, source_target_pairs={{0,8},{8,16},{16,24},{24,0},{1,9},{9,17},{17,25},{25,1},{2,10},{10... | collective-permute-start | bytes 73736 | tf_op jit(solution)/shard_map/ppermute | solution.py:16
  203.8 4.5 %collective-permute-start.37 = (f32[3,2,8,128]{3,2,1,0:T(8,128)S(1)}, f32[3,2,8,128]{3,2,1,0:T(8,128)S(1)}, u32[]{:S(2)}, u32[]{:S(2)}) collective-permute-start(f32[3,2,8,128]{3,2,1,0:T(8,128)S(1)} %get-tuple-element.296), channel_id=1, source_target_pairs={{8,0},{16,8},{24,16},{0,24},{9,1},{17,9},{25,17},{1,25},{10,2},{18... | collective-permute-start | bytes 73736 | tf_op jit(solution)/shard_map/ppermute | solution.py:18
  213.6 8.0 %collective-permute-start.40 = (f32[3,12,12,2]{3,2,1,0:T(8,128)S(1)}, f32[3,12,12,2]{3,2,1,0:T(8,128)S(1)}, u32[]{:S(2)}, u32[]{:S(2)}) collective-permute-start(f32[3,12,12,2]{3,2,1,0:T(8,128)S(1)} %get-tuple-element.279), channel_id=1, source_target_pairs={{0,1},{1,2},{2,3},{3,0},{4,5},{5,6},{6,7},{7,4},{8,9},{9,10},{10,1... | collective-permute-start | bytes 10376 | tf_op jit(solution)/shard_map/ppermute | solution.py:16
  213.7 8.0 %collective-permute-start.41 = (f32[3,12,12,2]{3,2,1,0:T(8,128)S(1)}, f32[3,12,12,2]{3,2,1,0:T(8,128)S(1)}, u32[]{:S(2)}, u32[]{:S(2)}) collective-permute-start(f32[3,12,12,2]{3,2,1,0:T(8,128)S(1)} %get-tuple-element.280), channel_id=1, source_target_pairs={{1,0},{2,1},{3,2},{0,3},{5,4},{6,5},{7,6},{4,7},{9,8},{10,9},{11,1... | collective-permute-start | bytes 10376 | tf_op jit(solution)/shard_map/ppermute | solution.py:18
  267.6 6.9 %collective-permute-start.42 = (f32[3,2,12,132]{3,2,1,0:T(8,128)S(1)}, f32[3,2,12,132]{3,2,1,0:T(8,128)S(1)}, u32[]{:S(2)}, u32[]{:S(2)}) collective-permute-start(f32[3,2,12,132]{3,2,1,0:T(8,128)S(1)} %get-tuple-element.265), channel_id=1, source_target_pairs={{0,8},{8,16},{16,24},{24,0},{1,9},{9,17},{17,25},{25,1},{2,10},{10... | collective-permute-start | bytes 114056 | tf_op jit(solution)/shard_map/ppermute | solution.py:16
  269.8 5.6 %collective-permute-start.43 = (f32[3,2,12,132]{3,2,1,0:T(8,128)S(1)}, f32[3,2,12,132]{3,2,1,0:T(8,128)S(1)}, u32[]{:S(2)}, u32[]{:S(2)}) collective-permute-start(f32[3,2,12,132]{3,2,1,0:T(8,128)S(1)} %get-tuple-element.266), channel_id=1, source_target_pairs={{8,0},{16,8},{24,16},{0,24},{9,1},{17,9},{25,17},{1,25},{10,2},{18... | collective-permute-start | bytes 114056 | tf_op jit(solution)/shard_map/ppermute | solution.py:18
  275.5 5.0 %collective-permute-start.44 = (f32[3,16,2,132]{3,2,1,0:T(2,128)S(1)}, f32[3,16,2,132]{3,2,1,0:T(2,128)S(1)}, u32[]{:S(2)}, u32[]{:S(2)}) collective-permute-start(f32[3,16,2,132]{3,2,1,0:T(2,128)S(1)} %get-tuple-element.205), channel_id=1, source_target_pairs={{0,4},{4,0},{1,5},{5,1},{2,6},{6,2},{3,7},{7,3},{8,12},{12,8},{9,1... | collective-permute-start | bytes 152072 | tf_op jit(solution)/shard_map/ppermute | solution.py:16
  277.7 4.6 %collective-permute-start.45 = (f32[3,16,2,132]{3,2,1,0:T(2,128)S(1)}, f32[3,16,2,132]{3,2,1,0:T(2,128)S(1)}, u32[]{:S(2)}, u32[]{:S(2)}) collective-permute-start(f32[3,16,2,132]{3,2,1,0:T(2,128)S(1)} %get-tuple-element.206), channel_id=1, source_target_pairs={{4,0},{0,4},{5,1},{1,5},{6,2},{2,6},{7,3},{3,7},{12,8},{8,12},{13,... | collective-permute-start | bytes 152072 | tf_op jit(solution)/shard_map/ppermute | solution.py:18
  282.7 10.2 %collective-permute-start.46 = (f32[3,16,16,2]{3,2,1,0:T(8,128)S(1)}, f32[3,16,16,2]{3,2,1,0:T(8,128)S(1)}, u32[]{:S(2)}, u32[]{:S(2)}) collective-permute-start(f32[3,16,16,2]{3,2,1,0:T(8,128)S(1)} %get-tuple-element.203), channel_id=1, source_target_pairs={{0,1},{1,2},{2,3},{3,0},{4,5},{5,6},{6,7},{7,4},{8,9},{9,10},{10,1... | collective-permute-start | bytes 18440 | tf_op jit(solution)/shard_map/ppermute | solution.py:16
  282.8 10.1 %collective-permute-start.47 = (f32[3,16,16,2]{3,2,1,0:T(8,128)S(1)}, f32[3,16,16,2]{3,2,1,0:T(8,128)S(1)}, u32[]{:S(2)}, u32[]{:S(2)}) collective-permute-start(f32[3,16,16,2]{3,2,1,0:T(8,128)S(1)} %get-tuple-element.204), channel_id=1, source_target_pairs={{1,0},{2,1},{3,2},{0,3},{5,4},{6,5},{7,6},{4,7},{9,8},{10,9},{11,1... | collective-permute-start | bytes 18440 | tf_op jit(solution)/shard_map/ppermute | solution.py:18
  294.6 7.0 %collective-permute-start.48 = (f32[18,1,8,128]{3,2,1,0:T(8,128)S(1)}, f32[18,1,8,128]{3,2,1,0:T(8,128)S(1)}, u32[]{:S(2)}, u32[]{:S(2)}) collective-permute-start(f32[18,1,8,128]{3,2,1,0:T(8,128)S(1)} %get-tuple-element.263), channel_id=1, source_target_pairs={{0,8},{8,16},{16,24},{24,0},{1,9},{9,17},{17,25},{25,1},{2,10},{10... | collective-permute-start | bytes 221192 | tf_op jit(solution)/shard_map/ppermute | solution.py:16
  295.4 6.6 %collective-permute-start.49 = (f32[18,1,8,128]{3,2,1,0:T(8,128)S(1)}, f32[18,1,8,128]{3,2,1,0:T(8,128)S(1)}, u32[]{:S(2)}, u32[]{:S(2)}) collective-permute-start(f32[18,1,8,128]{3,2,1,0:T(8,128)S(1)} %get-tuple-element.264), channel_id=1, source_target_pairs={{8,0},{16,8},{24,16},{0,24},{9,1},{17,9},{25,17},{1,25},{10,2},{18... | collective-permute-start | bytes 221192 | tf_op jit(solution)/shard_map/ppermute | solution.py:18
  302.1 5.6 %collective-permute-start.50 = (f32[18,10,1,128]{3,2,1,0:T(1,128)S(1)}, f32[18,10,1,128]{3,2,1,0:T(1,128)S(1)}, u32[]{:S(2)}, u32[]{:S(2)}) collective-permute-start(f32[18,10,1,128]{3,2,1,0:T(1,128)S(1)} %get-tuple-element.219), channel_id=1, source_target_pairs={{4,0},{0,4},{5,1},{1,5},{6,2},{2,6},{7,3},{3,7},{12,8},{8,12},{13,... | collective-permute-start | bytes 276488 | tf_op jit(solution)/shard_map/ppermute | solution.py:18
  303.2 5.4 %collective-permute-start.51 = (f32[18,10,1,128]{3,2,1,0:T(1,128)S(1)}, f32[18,10,1,128]{3,2,1,0:T(1,128)S(1)}, u32[]{:S(2)}, u32[]{:S(2)}) collective-permute-start(f32[18,10,1,128]{3,2,1,0:T(1,128)S(1)} %get-tuple-element.220), channel_id=1, source_target_pairs={{0,4},{4,0},{1,5},{5,1},{2,6},{6,2},{3,7},{7,3},{8,12},{12,8},{9,1... | collective-permute-start | bytes 276488 | tf_op jit(solution)/shard_map/ppermute | solution.py:16
  321.3 5.7 %collective-permute-start.54 = (f32[3,2,8,128]{3,2,1,0:T(8,128)S(1)}, f32[3,2,8,128]{3,2,1,0:T(8,128)S(1)}, u32[]{:S(2)}, u32[]{:S(2)}) collective-permute-start(f32[3,2,8,128]{3,2,1,0:T(8,128)S(1)} %get-tuple-element.293), channel_id=1, source_target_pairs={{0,8},{8,16},{16,24},{24,0},{1,9},{9,17},{17,25},{25,1},{2,10},{10... | collective-permute-start | bytes 73736 | tf_op jit(solution)/shard_map/ppermute | solution.py:16
  322.7 4.3 %collective-permute-start.55 = (f32[3,2,8,128]{3,2,1,0:T(8,128)S(1)}, f32[3,2,8,128]{3,2,1,0:T(8,128)S(1)}, u32[]{:S(2)}, u32[]{:S(2)}) collective-permute-start(f32[3,2,8,128]{3,2,1,0:T(8,128)S(1)} %get-tuple-element.294), channel_id=1, source_target_pairs={{8,0},{16,8},{24,16},{0,24},{9,1},{17,9},{25,17},{1,25},{10,2},{18... | collective-permute-start | bytes 73736 | tf_op jit(solution)/shard_map/ppermute | solution.py:18
  332.4 7.9 %collective-permute-start.58 = (f32[3,12,12,2]{3,2,1,0:T(8,128)S(1)}, f32[3,12,12,2]{3,2,1,0:T(8,128)S(1)}, u32[]{:S(2)}, u32[]{:S(2)}) collective-permute-start(f32[3,12,12,2]{3,2,1,0:T(8,128)S(1)} %get-tuple-element.277), channel_id=1, source_target_pairs={{0,1},{1,2},{2,3},{3,0},{4,5},{5,6},{6,7},{7,4},{8,9},{9,10},{10,1... | collective-permute-start | bytes 10376 | tf_op jit(solution)/shard_map/ppermute | solution.py:16
  332.4 8.0 %collective-permute-start.59 = (f32[3,12,12,2]{3,2,1,0:T(8,128)S(1)}, f32[3,12,12,2]{3,2,1,0:T(8,128)S(1)}, u32[]{:S(2)}, u32[]{:S(2)}) collective-permute-start(f32[3,12,12,2]{3,2,1,0:T(8,128)S(1)} %get-tuple-element.278), channel_id=1, source_target_pairs={{1,0},{2,1},{3,2},{0,3},{5,4},{6,5},{7,6},{4,7},{9,8},{10,9},{11,1... | collective-permute-start | bytes 10376 | tf_op jit(solution)/shard_map/ppermute | solution.py:18
  (30 other events, 269.0 us)
where the time goes:
time: 387 us; the launch traced here: 386 us
  waiting for transfers between devices  125 us (32%)
  blocking collectives  119 us (31%)
  starting transfers between devices  75.5 us (20%)
  local copies, waits for them, and re-layouts  34.9 us (9%)
  other arithmetic  14.6 us (4%)
  between operations  11.1 us (3%)
  matrix products  5.57 us (1%)
    psum x3, blocking collectives, both_products(): lax.psum((jnp.sum(vector * vector), jnp.sum(vector * image)), ('gx', 'gy'...  119 us
    ppermute x30, waiting for transfers between devices, extended(): lax.ppermute(tail, axis, [(i, (i + 1) % count) for i in range(count)])  98.9 us
    ppermute x30, starting transfers between devices, extended(): lax.ppermute(head, axis, [((i + 1) % count, i) for i in range(count)])  44.6 us
    ppermute x30, starting transfers between devices, extended(): lax.ppermute(tail, axis, [(i, (i + 1) % count) for i in range(count)])  30.9 us
    ppermute x30, waiting for transfers between devices, extended(): lax.ppermute(head, axis, [((i + 1) % count, i) for i in range(count)])  26.5 us
    slice x6, local copies, waits for them, and re-layouts, extended(): head = lax.slice_in_dim(cells, 0, width, axis=dim)  11.1 us
  transfers between devices with their start and end apart: 60, of which 49 were waited for; matrix products, arithmetic and copies ran while one was open for 3% of the time, Pallas kernels for 0%

commit v1 on v0

v1 whole, which is shorter than its diff:
```python
import functools
import itertools

import jax
import jax.numpy as jnp
from jax import lax
from jax.experimental import pallas as pl
from jax.experimental.pallas import tpu as pltpu
from jax.sharding import PartitionSpec as P

ITERS = 3
LOW, HIGH = 2, 3
MESH_ID = pl.DeviceIdType.MESH
AXES = ("gx", "gy", "gz")


def round_up(value, multiple):
    return -(-value // multiple) * multiple


def extended(cells, sides):
    for axis, dim in sides:
        count = lax.axis_size(axis)
        head = lax.slice_in_dim(cells, 0, HIGH, axis=dim)
        tail = lax.slice_in_dim(cells, cells.shape[dim] - LOW, cells.shape[dim], axis=dim)
        cells = jnp.concatenate(
            [
                lax.ppermute(tail, axis, [(i, (i + 1) % count) for i in range(count)]),
                cells,
                lax.ppermute(head, axis, [((i + 1) % count, i) for i in range(count)]),
            ],
            axis=dim,
        )
    return cells


def axis_groups(count):
    groups = {}
    for shift in (0, -1, 1):
        groups.setdefault(shift % count, []).append(shift)
    return list(groups.items())


def span(shifts, size):
    if shifts == [0]:
        return 1, size + 3
    if shifts == [-1]:
        return 0, 4
    if shifts == [1]:
        return size + 1, 4
    return 0, size + 5


def weights(fraction):
    root = jnp.sqrt(1.0 + 4.0 * fraction - 4.0 * fraction * fraction)
    near, far = 3.0 - 2.0 * fraction, 1.0 + 2.0 * fraction
    return ((near - root) / 8.0, (near + root) / 8.0, (far + root) / 8.0, (far - root) / 8.0)


def table(cell, four, shifts, size, first, rows):
    place = lax.broadcasted_iota(jnp.int32, (rows, cell.shape[1]), 0).astype(jnp.float32) + first
    total = None
    for shift in shifts:
        apart = place - (cell + (1.0 + shift * size))
        part = jnp.where(apart == 3.0, four[3], 0.0)
        for number in (2, 1, 0):
            part = jnp.where(apart == float(number), four[number], part)
        total = part if total is None else total + part
    return total


def split(value):
    high = value.astype(jnp.bfloat16)
    return high, (value - high.astype(jnp.float32)).astype(jnp.bfloat16)


def dot_nt(a, b):
    return lax.dot_general(a, b, (((1,), (1,)), ((), ())), preferred_element_type=jnp.float32)


def dot_nn(a, b):
    return lax.dot_general(a, b, (((1,), (0,)), ((), ())), preferred_element_type=jnp.float32)


def kernel(
    counts, sizes, fields, marks, aux, out, nbuf, rbuf, txy, thi, tlo, whi, wlo, grid,
    nsend, nrecv, rsend, rrecv,
):
    size_x, size_y, size_z = sizes
    cap = marks.shape[1]
    rows_y, lanes = fields.shape[2], fields.shape[3]
    wide_x = size_x + 5
    groups = [axis_groups(count) for count in counts]
    slots = list(itertools.product(*[[offset for offset, _ in group] for group in groups]))
    me = [lax.axis_index(name) for name in AXES]
    sent = []

    def device(offset):
        return tuple(lax.rem(m + o, n) for m, o, n in zip(me, offset, counts))

    def negated(offset):
        return tuple((-o) % n for o, n in zip(offset, counts))

    peers = {slot for slot in slots if any(slot)}
    for axis, count in enumerate(counts):
        for step in range(1, count):
            peers.add(tuple(step if a == axis else 0 for a in range(3)))
    peers = sorted(peers)
    barrier = pltpu.get_barrier_semaphore()
    for peer in peers:
        pl.semaphore_signal(barrier, inc=1, device_id=device(peer), device_id_type=MESH_ID)
    pl.semaphore_wait(barrier, len(peers))

    def neighbour_copy(turn, number):
        return pltpu.make_async_remote_copy(
            src_ref=nbuf.at[turn, 0],
            dst_ref=nbuf.at[turn, number],
            send_sem=nsend.at[turn, number - 1],
            recv_sem=nrecv.at[turn, number - 1],
            device_id=device(negated(slots[number])),
            device_id_type=MESH_ID,
        )

    def send_round(turn):
        for number in range(1, len(slots)):
            copy = neighbour_copy(turn, number)
            copy.start()
            sent.append(copy)

    def wait_round(turn):
        for number in range(1, len(slots)):
            neighbour_copy(turn, number).wait_recv()

    def sum_copy(turn, stage, step):
        axis = 2 - stage
        offset = tuple((-step) % counts[axis] if a == axis else 0 for a in range(3))
        return pltpu.make_async_remote_copy(
            src_ref=rbuf.at[turn, stage, 0],
            dst_ref=rbuf.at[turn, stage, step],
            send_sem=rsend.at[turn, stage, step - 1],
            recv_sem=rrecv.at[turn, stage, step - 1],
            device_id=device(offset),
            device_id_type=MESH_ID,
        )

    def send_sum(turn, stage, value):
        rbuf[turn, stage, 0] = value
        for step in range(1, counts[2 - stage]):
            copy = sum_copy(turn, stage, step)
            copy.start()
            sent.append(copy)

    def wait_sum(turn, stage):
        for step in range(1, counts[2 - stage]):
            sum_copy(turn, stage, step).wait_recv()
        total = rbuf[turn, stage, 0]
        for step in range(1, counts[2 - stage]):
            total = total + rbuf[turn, stage, step]
        return total

    def put(turn, vector):
        for c in range(3):
            nbuf[turn, 0, pl.ds(c, 1), :] = vector[c : c + 1]

    nbuf[0, 0] = marks[...]
    send_round(0)

    def build(xi, yi, zi):
        number = slots.index((groups[0][xi][0], groups[1][yi][0], groups[2][zi][0]))
        info = nbuf[0, number]
        cells = [info[k : k + 1] for k in range(3)]
        fours = [weights(info[k + 3 : k + 4]) for k in range(3)]
        block = (yi * len(groups[2]) + zi) * cap
        start, planes = span(groups[0][xi][1], size_x)
        first = start // 8 * 8
        tall = round_up(start + planes - first, 8)
        tab_x = table(cells[0], fours[0], groups[0][xi][1], size_x, float(first), tall)
        tab_y = table(cells[1], fours[1], groups[1][yi][1], size_y, 0.0, rows_y)
        for plane in range(planes):
            at = start - first + plane
            txy[xi, pl.ds(plane * rows_y, rows_y), pl.ds(block, cap)] = tab_x[at : at + 1] * tab_y
        shifts = groups[2][zi][1]
        start, planes = span(shifts, size_z)
        first = start // 16 * 16
        tall = round_up(start + planes - first, 16)
        tab_z = table(cells[2], fours[2], shifts, size_z, float(first), tall)
        high, low = split(tab_z)
        for ref, part in ((thi, high), (tlo, low)):
            if first:
                ref[xi, pl.ds(0, first), pl.ds(block, cap)] = jnp.zeros((first, cap), jnp.bfloat16)
            ref[xi, pl.ds(first, tall), pl.ds(block, cap)] = part
            rest = lanes - first - tall
            if rest:
                ref[xi, pl.ds(first + tall, rest), pl.ds(block, cap)] = jnp.zeros(
                    (rest, cap), jnp.bfloat16
                )

    start_own, planes_own = span(groups[0][0][1], size_x)

    def interpolate(field):
        rows = planes_own * rows_y
        high, low = split(field.reshape(3 * rows, lanes))
        z_high, z_low = thi[0, :, pl.ds(0, cap)], tlo[0, :, pl.ds(0, cap)]
        part = dot_nn(high, z_high) + dot_nn(low, z_high) + dot_nn(high, z_low)
        plane = txy[0, pl.ds(0, rows), pl.ds(0, cap)]
        return jnp.concatenate(
            [
                jnp.sum(part[c * rows : (c + 1) * rows] * plane, axis=0, keepdims=True)
                for c in range(3)
            ],
            axis=0,
        )

    def spread(turn):
        for xi, (off_x, shifts) in enumerate(groups[0]):
            start, planes = span(shifts, size_x)
            rows = planes * rows_y
            for yi, (off_y, _) in enumerate(groups[1]):
                for zi, (off_z, _) in enumerate(groups[2]):
                    number = slots.index((off_x, off_y, off_z))
                    block = (yi * len(groups[2]) + zi) * cap
                    plane = txy[xi, pl.ds(0, rows), pl.ds(block, cap)]
                    for c in range(3):
                        high, low = split(plane * nbuf[turn, number, pl.ds(c, 1), :])
                        whi[pl.ds(c * rows, rows), pl.ds(block, cap)] = high
                        wlo[pl.ds(c * rows, rows), pl.ds(block, cap)] = low
            high, low = whi[pl.ds(0, 3 * rows), :], wlo[pl.ds(0, 3 * rows), :]
            part = dot_nt(high, thi[xi]) + dot_nt(low, thi[xi]) + dot_nt(high, tlo[xi])
            part = part.reshape(3, planes, rows_y, lanes)
            if xi == 0:
                if start > 0:
                    grid[:, pl.ds(0, start)] = jnp.zeros((3, start, rows_y, lanes), jnp.float32)
                rest = wide_x - start - planes
                if rest > 0:
                    grid[:, pl.ds(start + planes, rest)] = jnp.zeros(
                        (3, rest, rows_y, lanes), jnp.float32
                    )
                grid[:, pl.ds(start, planes)] = part
            else:
                grid[:, pl.ds(start, planes)] += part

    def shifted(value, by, axis):
        return pltpu.roll(value, by % value.shape[axis], axis)

    def both(value, axis):
        return shifted(value, -1, axis), shifted(value, 1, axis)

    def add(value, axis):
        up, down = both(value, axis)
        return up + down

    def sub(value, axis):
        up, down = both(value, axis)
        return up - down

    def respond():
        scale = fields[3]
        mx, my, mz = (scale * grid[c] for c in range(3))
        slope_y, slope_z = sub(my, 1), sub(mz, 2)
        sum_x = 2.0 * mx + add(mx, 1) + add(mx, 2)
        slope = slope_y + slope_z
        px = sum_x[2:] + sum_x[:-2] + slope[2:] - slope[:-2]
        slope_x = mx[2:] - mx[:-2]
        sum_y = (2.0 * my + add(my, 2))[1:-1] + my[2:] + my[:-2]
        py = add(sum_y, 1) + sub(slope_x + slope_z[1:-1], 1)
        sum_z = (2.0 * mz + add(mz, 1))[1:-1] + mz[2:] + mz[:-2]
        pz = add(sum_z, 2) + sub(slope_x + slope_y[1:-1], 2)
        half = scale[1:-1] * 0.5
        return jnp.stack(
            [half * (m[1:-1] + p * (1.0 / 12.0)) for m, p in ((mx, px), (my, py), (mz, pz))]
        )

    target, stiffness, live = aux[pl.ds(0, 3), :], aux[pl.ds(3, 1), :], aux[pl.ds(4, 1), :]

    def apply(turn, vector, summing=None):
        wait_round(turn)
        spread(turn)
        if summing is not None:
            send_sum(summing, 1, wait_sum(summing, 0))
        field = respond()
        if summing is not None:
            send_sum(summing, 2, wait_sum(summing, 1))
        return live * (interpolate(field) + stiffness * vector)

    def partial_sums(residual, image):
        folded = []
        for other in (residual, image):
            row = jnp.sum(residual * other, axis=0, keepdims=True)
            total = row[:, :128]
            for at in range(128, cap, 128):
                total = total + row[:, at : at + 128]
            folded.append(total)
        which = lax.broadcasted_iota(jnp.int32, (8, 128), 0)
        return jnp.where(which == 0, folded[0], jnp.where(which == 1, folded[1], 0.0))

    def totals(turn):
        tile = wait_sum(turn, 2)
        return (
            jnp.sum(tile[0:1], axis=1, keepdims=True),
            jnp.sum(tile[1:2], axis=1, keepdims=True),
        )

    build(0, 0, 0)
    residual = live * (target - interpolate(fields[pl.ds(0, 3), pl.ds(1, size_x + 3)]))
    put(1, residual)
    send_round(1)
    wait_round(0)
    for xi, yi, zi in itertools.product(*[range(len(group)) for group in groups]):
        if (xi, yi, zi) != (0, 0, 0):
            build(xi, yi, zi)

    image = apply(1, residual)
    direction, along, along_image = residual, image, None
    answer = None
    norm_before = alpha = None
    for step in range(ITERS):
        send_sum(step, 0, partial_sums(residual, image))
        if step + 1 < ITERS:
            put(step + 2, image)
            send_round(step + 2)
            ahead = apply(step + 2, image, step)
        else:
            send_sum(step, 1, wait_sum(step, 0))
            send_sum(step, 2, wait_sum(step, 1))
        norm, product = totals(step)
        if step == 0:
            alpha = norm / product
            along_image = ahead
        else:
            ratio = norm / norm_before
            alpha = norm / (product - ratio * norm / alpha)
            direction = residual + ratio * direction
            if step + 1 < ITERS:
                along = image + ratio * along
                along_image = ahead + ratio * along_image
        answer = alpha * direction if answer is None else answer + alpha * direction
        norm_before = norm
        if step + 1 < ITERS:
            residual = residual - alpha * along
            image = image - alpha * along_image
    out[...] = answer
    for copy in sent:
        copy.wait_send()


def body(mesh_counts, density, base_velocity, cells, offsets, target, stiffness, counts):
    sizes = density.shape
    size_x, size_y, size_z = sizes
    cap = cells.shape[1]
    rows_y, lanes = round_up(size_y + 5, 16), round_up(size_z + 5, 128)
    anchor = jnp.stack([lax.axis_index(name) * size for name, size in zip(AXES, sizes)])
    local = (cells - anchor[:, None]).astype(jnp.float32)
    marks = jnp.concatenate([local, offsets, jnp.zeros((2, cap), jnp.float32)], axis=0)
    live = (jnp.arange(cap, dtype=jnp.int32) < counts[0]).astype(jnp.float32)
    aux = jnp.concatenate(
        [target, stiffness[None], live[None], jnp.zeros((3, cap), jnp.float32)], axis=0
    )
    stacked = jnp.concatenate([base_velocity, lax.rsqrt(density)[None]], axis=0)
    fields = extended(stacked, (("gz", 3), ("gy", 2), ("gx", 1)))
    fields = jnp.pad(
        fields, ((0, 0), (0, 0), (0, rows_y - size_y - 5), (0, lanes - size_z - 5))
    )
    groups = [axis_groups(count) for count in mesh_counts]
    number = len(groups[0]) * len(groups[1]) * len(groups[2])
    width = len(groups[1]) * len(groups[2]) * cap
    tallest = max(span(shifts, size_x)[1] for _, shifts in groups[0])
    longest = max(mesh_counts)
    turns = ITERS + 1
    return pl.pallas_call(
        functools.partial(kernel, mesh_counts, sizes),
        out_shape=jax.ShapeDtypeStruct((3, cap), jnp.float32),
        in_specs=[pl.BlockSpec(memory_space=pltpu.VMEM)] * 3,
        out_specs=pl.BlockSpec(memory_space=pltpu.VMEM),
        scratch_shapes=[
            pltpu.VMEM((turns, number, 8, cap), jnp.float32),
            pltpu.VMEM((ITERS, 3, longest, 8, 128), jnp.float32),
            pltpu.VMEM((len(groups[0]), tallest * rows_y, width), jnp.float32),
            pltpu.VMEM((len(groups[0]), lanes, width), jnp.bfloat16),
            pltpu.VMEM((len(groups[0]), lanes, width), jnp.bfloat16),
            pltpu.VMEM((3 * tallest * rows_y, width), jnp.bfloat16),
            pltpu.VMEM((3 * tallest * rows_y, width), jnp.bfloat16),
            pltpu.VMEM((3, size_x + 5, rows_y, lanes), jnp.float32),
            pltpu.SemaphoreType.DMA((turns, number - 1)),
            pltpu.SemaphoreType.DMA((turns, number - 1)),
            pltpu.SemaphoreType.DMA((ITERS, 3, longest - 1)),
            pltpu.SemaphoreType.DMA((ITERS, 3, longest - 1)),
        ],
        compiler_params=pltpu.CompilerParams(
            collective_id=0, has_side_effects=True, vmem_limit_bytes=60 * 1024 * 1024
        ),
    )(fields, marks, aux)


def solution(mesh):
    return jax.shard_map(
        functools.partial(body, tuple(mesh.shape[name] for name in AXES)),
        mesh=mesh,
        in_specs=(
            P("gx", "gy", "gz"),
            P(None, "gx", "gy", "gz"),
            P(None, ("gx", "gy", "gz")),
            P(None, ("gx", "gy", "gz")),
            P(None, ("gx", "gy", "gz")),
            P(("gx", "gy", "gz")),
            P(("gx", "gy", "gz")),
        ),
        out_specs=P(None, ("gx", "gy", "gz")),
        check_vma=False,
    )
```

time: 387 us -> 90.6 us (0.23)
  blocking collectives: 119 us -> 0 us
  waiting for transfers between devices: 125 us -> 14 us
  starting transfers between devices: 75.5 us -> 8.62 us
  Pallas kernels: 0 us -> 60.4 us
  local copies, waits for them, and re-layouts: 34.9 us -> 3.84 us
  other arithmetic: 14.6 us -> 2.76 us
  between operations: 11.1 us -> 0.73 us
  matrix products: 5.57 us -> 0 us
    psum x3 -> x0, blocking collectives: 119 us -> none  [both_products(): lax.psum((jnp.sum(vector * vector), jnp.sum(vector * image)), ('gx', 'gy'...]
    ppermute x30 -> x3, waiting for transfers between devices: 98.9 us -> 9.66 us  [extended(): lax.ppermute(tail, axis, [(i, (i + 1) % count) for i in range(count)])]
    pallas_call x0 -> x1, Pallas kernels: none -> 60.4 us  [body(): pl.pallas_call(functools.partial(kernel, mesh_counts, sizes), out_shape=j...]
    ppermute x30 -> x3, starting transfers between devices: 44.6 us -> 5.88 us  [extended(): lax.ppermute(head, axis, [((i + 1) % count, i) for i in range(count)])]
    ppermute x30 -> x3, starting transfers between devices: 30.9 us -> 2.74 us  [extended(): lax.ppermute(tail, axis, [(i, (i + 1) % count) for i in range(count)])]
    ppermute x30 -> x3, waiting for transfers between devices: 26.5 us -> 4.3 us  [extended(): lax.ppermute(head, axis, [((i + 1) % count, i) for i in range(count)])]
    slice x33 -> x0, local copies, waits for them, and re-layouts: 15 us -> none  [the longest x6 11.1 us: extended(): head = lax.slice_in_dim(cells, 0, width, axis=dim)]
    ppermute x6 -> x0, local copies, waits for them, and re-layouts: 11.7 us -> none  [the longest x3 7.05 us: extended(): lax.ppermute(tail, axis, [(i, (i + 1) % count) for i in range(count)])]
  transfers between devices with their start and end apart: 60 -> 6, of which waited for: 49 -> 5; matrix products, arithmetic and copies ran while one was open for 3% -> 1% of each run, Pallas kernels for 0% -> 0%
where the time goes in v1:
time: 90.6 us; the launch traced here: 90.3 us
  Pallas kernels  60.4 us (67%)
  waiting for transfers between devices  14 us (15%)
  starting transfers between devices  8.62 us (10%)
  local copies, waits for them, and re-layouts  3.84 us (4%)
  other arithmetic  2.76 us (3%)
    pallas_call x1, Pallas kernels, body(): pl.pallas_call(functools.partial(kernel, mesh_counts, sizes), out_shape=j...  60.4 us
    ppermute x3, waiting for transfers between devices, extended(): lax.ppermute(tail, axis, [(i, (i + 1) % count) for i in range(count)])  9.66 us
    ppermute x3, starting transfers between devices, extended(): lax.ppermute(head, axis, [((i + 1) % count, i) for i in range(count)])  5.88 us
    ppermute x3, waiting for transfers between devices, extended(): lax.ppermute(head, axis, [((i + 1) % count, i) for i in range(count)])  4.3 us
    ppermute x3, starting transfers between devices, extended(): lax.ppermute(tail, axis, [(i, (i + 1) % count) for i in range(count)])  2.74 us
    unnamed x11, local copies, waits for them, and re-layouts  1.9 us
  transfers between devices with their start and end apart: 6, of which 5 were waited for; matrix products, arithmetic and copies ran while one was open for 1% of the time, Pallas kernels for 0%

profile of v1, /device:TPU:0, one launch (start us, length us, event | category | flops | bytes accessed | tf_op | source)
XLA Modules:
  0.0 90.3 jit_solution(12460249180825615084)
XLA Ops:
  0.0 0.8 rsqrt_bitcast_fusion
  0.8 0.0 copy-start
  0.8 1.0 %slice_maximum_fusion = f32[4,8,8,2]{3,2,1,0:T(8,128)S(1)} fusion(f32[1,8,8,128]{3,2,1,0:T(8,128)S(1)} %rsqrt_bitcast_fusion, f32[3,8,8,128]{3,2,1,0:T(8,128)} %param.8), kind=kLoop, calls=%fused_computation.11 | loop fusion | flops 512 | bytes 133120 | tf_op jit(solution)/shard_map/concatenate | solution.py:358
  1.8 0.5 collective-permute-start
  2.4 0.0 copy-done
  2.4 2.0 %collective-permute-start.1 = (f32[4,8,8,3]{3,2,1,0:T(8,128)S(1)}, f32[4,8,8,3]{3,2,1,0:T(8,128)S(1)}, u32[]{:S(2)}, u32[]{:S(2)}) collective-permute-start(f32[4,8,8,3]{3,2,1,0:T(8,128)S(1)} %pad_maximum_fusion.10), channel_id=1, source_target_pairs={{1,0},{2,1},{3,2},{0,3},{5,4},{6,5},{7,6},{4,7},{9,8},{10,9},{11,1... | collective-permute-start | bytes 9224 | tf_op jit(solution)/shard_map/ppermute | solution.py:30
  4.4 0.0 copy-start.1
  4.4 0.1 pad_add_fusion
  4.5 0.6 copy-done.1
  5.1 0.1 subtract_convert_fusion
  5.8 1.1 %collective-permute-done = f32[4,8,8,2]{3,2,1,0:T(8,128)S(1)} collective-permute-done((f32[4,8,8,2]{3,2,1,0:T(8,128)S(1)}, f32[4,8,8,2]{3,2,1,0:T(8,128)S(1)}, u32[]{:S(2)}, u32[]{:S(2)}) %collective-permute-start) | collective-permute-done | bytes 2080 | tf_op jit(solution)/shard_map/ppermute | solution.py:28
  6.9 1.2 %collective-permute-done.1 = f32[4,8,8,3]{3,2,1,0:T(8,128)S(1)} collective-permute-done((f32[4,8,8,3]{3,2,1,0:T(8,128)S(1)}, f32[4,8,8,3]{3,2,1,0:T(8,128)S(1)}, u32[]{:S(2)}, u32[]{:S(2)}) %collective-permute-start.1) | collective-permute-done | bytes 3104 | tf_op jit(solution)/shard_map/ppermute | solution.py:30
  8.2 0.2 pad_maximum_fusion.7
  8.3 1.6 %collective-permute-start.3 = (f32[4,8,3,133]{3,2,1,0:T(4,128)S(1)}, f32[4,8,3,133]{3,2,1,0:T(4,128)S(1)}, u32[]{:S(2)}, u32[]{:S(2)}) collective-permute-start(f32[4,8,3,133]{3,2,1,0:T(4,128)S(1)} %pad_maximum_fusion.7), channel_id=1, source_target_pairs={{4,0},{0,4},{5,1},{1,5},{6,2},{2,6},{7,3},{3,7},{12,8},{8,12},{13,... | collective-permute-start | bytes 153224 | tf_op jit(solution)/shard_map/ppermute | solution.py:30
  9.9 0.2 pad_maximum_fusion.11
  10.1 0.6 collective-permute-start.2
  10.7 0.1 pad.11.clone
  10.8 0.1 pad.8.clone
  10.8 5.1 %collective-permute-done.2 = f32[4,8,2,133]{3,2,1,0:T(2,128)S(1)} collective-permute-done((f32[4,8,2,133]{3,2,1,0:T(2,128)S(1)}, f32[4,8,2,133]{3,2,1,0:T(2,128)S(1)}, u32[]{:S(2)}, u32[]{:S(2)}) %collective-permute-start.2) | collective-permute-done | bytes 34080 | tf_op jit(solution)/shard_map/ppermute | solution.py:28
  15.9 0.0 collective-permute-done.3
  15.9 0.1 pad_maximum_fusion.6
  16.0 1.6 %collective-permute-start.4 = (f32[4,2,13,133]{3,2,1,0:T(8,128)S(1)}, f32[4,2,13,133]{3,2,1,0:T(8,128)S(1)}, u32[]{:S(2)}, u32[]{:S(2)}) collective-permute-start(f32[4,2,13,133]{3,2,1,0:T(8,128)S(1)} %pad_maximum_fusion.6), channel_id=1, source_target_pairs={{0,8},{8,16},{16,24},{24,0},{1,9},{9,17},{17,25},{25,1},{2,10},{10... | collective-permute-start | bytes 165992 | tf_op jit(solution)/shard_map/ppermute | solution.py:28
  17.7 0.0 copy-start.2
  17.7 0.0 copy-start.3
  17.7 0.1 pad_maximum_fusion.1
  17.8 0.0 copy-start.4
  17.8 2.3 %collective-permute-start.5 = (f32[4,3,13,133]{3,2,1,0:T(8,128)S(1)}, f32[4,3,13,133]{3,2,1,0:T(8,128)S(1)}, u32[]{:S(2)}, u32[]{:S(2)}) collective-permute-start(f32[4,3,13,133]{3,2,1,0:T(8,128)S(1)} %pad_maximum_fusion.1), channel_id=1, source_target_pairs={{8,0},{16,8},{24,16},{0,24},{9,1},{17,9},{25,17},{1,25},{10,2},{18... | collective-permute-start | bytes 248984 | tf_op jit(solution)/shard_map/ppermute | solution.py:30
  20.1 0.0 copy-done.2
  20.1 0.0 copy-done.3
  20.1 0.0 copy-done.4
  20.1 0.7 maximum_maximum_fusion
  20.8 3.5 %collective-permute-done.4 = f32[4,2,13,133]{3,2,1,0:T(8,128)S(1)} collective-permute-done((f32[4,2,13,133]{3,2,1,0:T(8,128)S(1)}, f32[4,2,13,133]{3,2,1,0:T(8,128)S(1)}, u32[]{:S(2)}, u32[]{:S(2)}) %collective-permute-start.4) | collective-permute-done | bytes 55360 | tf_op jit(solution)/shard_map/ppermute | solution.py:28
  24.2 3.1 %collective-permute-done.5 = f32[4,3,13,133]{3,2,1,0:T(8,128)S(1)} collective-permute-done((f32[4,3,13,133]{3,2,1,0:T(8,128)S(1)}, f32[4,3,13,133]{3,2,1,0:T(8,128)S(1)}, u32[]{:S(2)}, u32[]{:S(2)}) %collective-permute-start.5) | collective-permute-done | bytes 83024 | tf_op jit(solution)/shard_map/ppermute | solution.py:30
  27.3 0.3 pad_maximum_fusion
  27.6 1.0 %pad.4.fields = f32[4,13,16,256]{3,2,1,0:T(8,128)} pad(f32[4,13,13,133]{3,2,1,0:T(8,128)S(1)} %pad_maximum_fusion, f32[]{:T(128)} %constant.6.clone.1), padding=0_0x0_0x0_3x0_123 | pad | bytes 1211604 | tf_op jit(solution)/shard_map/jit(_pad)/pad | solution.py:360
  28.6 60.4 %shard_map.73 = f32[3,256]{1,0:T(4,128)} custom-call(f32[4,13,16,256]{3,2,1,0:T(8,128)} %pad.4.fields, f32[8,256]{1,0:T(8,128)} %get-tuple-element.5.marks, f32[8,256]{1,0:T(8,128)} %get-tuple-element.6.aux), custom_call_target="tpu_custom_call" | custom-call | tf_op jit(solution)/shard_map/pallas_call | solution.py:369
  89.0 1.3 %copy.10 = f32[3,256]{1,0:T(4,128)} copy(f32[3,256]{1,0:T(4,128)} %shard_map.73) | data formatting | bytes 6144
  (4 shorter events, 0.0 us)
Async XLA Ops:
  0.8 1.6 %copy-start = (f32[3,8,8,128]{3,2,1,0:T(8,128)S(1)}, f32[3,8,8,128]{3,2,1,0:T(8,128)}, u32[]{:S(2)}) copy-start(f32[3,8,8,128]{3,2,1,0:T(8,128)} %param.8) | copy-start | bytes 294916
  1.8 5.1 %collective-permute-start = (f32[4,8,8,2]{3,2,1,0:T(8,128)S(1)}, f32[4,8,8,2]{3,2,1,0:T(8,128)S(1)}, u32[]{:S(2)}, u32[]{:S(2)}) collective-permute-start(f32[4,8,8,2]{3,2,1,0:T(8,128)S(1)} %slice_maximum_fusion), channel_id=1, source_target_pairs={{0,1},{1,2},{2,3},{3,0},{4,5},{5,6},{6,7},{7,4},{8,9},{9,10},{10,1... | collective-permute-start | bytes 6152 | tf_op jit(solution)/shard_map/ppermute | solution.py:28
  2.4 5.8 %collective-permute-start.1 = (f32[4,8,8,3]{3,2,1,0:T(8,128)S(1)}, f32[4,8,8,3]{3,2,1,0:T(8,128)S(1)}, u32[]{:S(2)}, u32[]{:S(2)}) collective-permute-start(f32[4,8,8,3]{3,2,1,0:T(8,128)S(1)} %pad_maximum_fusion.10), channel_id=1, source_target_pairs={{1,0},{2,1},{3,2},{0,3},{5,4},{6,5},{7,6},{4,7},{9,8},{10,9},{11,1... | collective-permute-start | bytes 9224 | tf_op jit(solution)/shard_map/ppermute | solution.py:30
  4.4 0.7 copy-start.1
  8.3 7.6 %collective-permute-start.3 = (f32[4,8,3,133]{3,2,1,0:T(4,128)S(1)}, f32[4,8,3,133]{3,2,1,0:T(4,128)S(1)}, u32[]{:S(2)}, u32[]{:S(2)}) collective-permute-start(f32[4,8,3,133]{3,2,1,0:T(4,128)S(1)} %pad_maximum_fusion.7), channel_id=1, source_target_pairs={{4,0},{0,4},{5,1},{1,5},{6,2},{2,6},{7,3},{3,7},{12,8},{8,12},{13,... | collective-permute-start | bytes 153224 | tf_op jit(solution)/shard_map/ppermute | solution.py:30
  10.1 5.8 %collective-permute-start.2 = (f32[4,8,2,133]{3,2,1,0:T(2,128)S(1)}, f32[4,8,2,133]{3,2,1,0:T(2,128)S(1)}, u32[]{:S(2)}, u32[]{:S(2)}) collective-permute-start(f32[4,8,2,133]{3,2,1,0:T(2,128)S(1)} %pad_maximum_fusion.11), channel_id=1, source_target_pairs={{0,4},{4,0},{1,5},{5,1},{2,6},{6,2},{3,7},{7,3},{8,12},{12,8},{9,1... | collective-permute-start | bytes 102152 | tf_op jit(solution)/shard_map/ppermute | solution.py:28
  16.0 8.2 %collective-permute-start.4 = (f32[4,2,13,133]{3,2,1,0:T(8,128)S(1)}, f32[4,2,13,133]{3,2,1,0:T(8,128)S(1)}, u32[]{:S(2)}, u32[]{:S(2)}) collective-permute-start(f32[4,2,13,133]{3,2,1,0:T(8,128)S(1)} %pad_maximum_fusion.6), channel_id=1, source_target_pairs={{0,8},{8,16},{16,24},{24,0},{1,9},{9,17},{17,25},{25,1},{2,10},{10... | collective-permute-start | bytes 165992 | tf_op jit(solution)/shard_map/ppermute | solution.py:28
  17.7 2.5 %copy-start.2 = (f32[3,256]{1,0:T(4,128)S(1)}, f32[3,256]{1,0:T(4,128)}, u32[]{:S(2)}) copy-start(f32[3,256]{1,0:T(4,128)} %param.10) | copy-start | bytes 9220
  17.7 2.5 %copy-start.3 = (f32[3,256]{1,0:T(4,128)S(1)}, f32[3,256]{1,0:T(4,128)}, u32[]{:S(2)}) copy-start(f32[3,256]{1,0:T(4,128)} %param.11) | copy-start | bytes 9220
  17.8 2.3 %copy-start.4 = (f32[256]{0:T(256)S(1)}, f32[256]{0:T(256)}, u32[]{:S(2)}) copy-start(f32[256]{0:T(256)} %param.12) | copy-start | bytes 3076
  17.8 9.5 %collective-permute-start.5 = (f32[4,3,13,133]{3,2,1,0:T(8,128)S(1)}, f32[4,3,13,133]{3,2,1,0:T(8,128)S(1)}, u32[]{:S(2)}, u32[]{:S(2)}) collective-permute-start(f32[4,3,13,133]{3,2,1,0:T(8,128)S(1)} %pad_maximum_fusion.1), channel_id=1, source_target_pairs={{8,0},{16,8},{24,16},{0,24},{9,1},{17,9},{25,17},{1,25},{10,2},{18... | collective-permute-start | bytes 248984 | tf_op jit(solution)/shard_map/ppermute | solution.py:30

commit v2 on v1

--- a/solution.py
+++ b/solution.py
@@ -9,6 +9,7 @@
 from jax.sharding import PartitionSpec as P
 
 ITERS = 3
+MOST_DIRECT = 64
 LOW, HIGH = 2, 3
 MESH_ID = pl.DeviceIdType.MESH
 AXES = ("gx", "gy", "gz")
@@ -83,8 +84,8 @@
 
 
 def kernel(
-    counts, sizes, fields, marks, aux, out, nbuf, rbuf, txy, thi, tlo, whi, wlo, grid,
-    nsend, nrecv, rsend, rrecv,
+    counts, sizes, fields, marks, aux, out, nbuf, fbuf, rbuf, dbuf, txy, thi, tlo, whi, wlo, grid,
+    nsend, nrecv, rsend, rrecv, dsend, drecv,
 ):
     size_x, size_y, size_z = sizes
     cap = marks.shape[1]
@@ -105,7 +106,9 @@
     for axis, count in enumerate(counts):
         for step in range(1, count):
             peers.add(tuple(step if a == axis else 0 for a in range(3)))
-    peers = sorted(peers)
+    everyone = [o for o in itertools.product(*[range(n) for n in counts]) if any(o)]
+    direct = len(everyone) < MOST_DIRECT
+    peers = everyone if direct else sorted(peers)
     barrier = pltpu.get_barrier_semaphore()
     for peer in peers:
         pl.semaphore_signal(barrier, inc=1, device_id=device(peer), device_id_type=MESH_ID)
@@ -113,8 +116,8 @@
 
     def neighbour_copy(turn, number):
         return pltpu.make_async_remote_copy(
-            src_ref=nbuf.at[turn, 0],
-            dst_ref=nbuf.at[turn, number],
+            src_ref=fbuf.at[turn - 1, 0] if turn else nbuf.at[0],
+            dst_ref=fbuf.at[turn - 1, number] if turn else nbuf.at[number],
             send_sem=nsend.at[turn, number - 1],
             recv_sem=nrecv.at[turn, number - 1],
             device_id=device(negated(slots[number])),
@@ -122,14 +125,15 @@
         )
 
     def send_round(turn):
-        for number in range(1, len(slots)):
+        for number in sorted(range(1, len(slots)), key=lambda k: (slots[k][0] == 0, k)):
             copy = neighbour_copy(turn, number)
             copy.start()
             sent.append(copy)
 
-    def wait_round(turn):
+    def wait_round(turn, off_x):
         for number in range(1, len(slots)):
-            neighbour_copy(turn, number).wait_recv()
+            if slots[number][0] == off_x:
+                neighbour_copy(turn, number).wait_recv()
 
     def sum_copy(turn, stage, step):
         axis = 2 - stage
@@ -160,14 +164,43 @@
 
     def put(turn, vector):
         for c in range(3):
-            nbuf[turn, 0, pl.ds(c, 1), :] = vector[c : c + 1]
-
-    nbuf[0, 0] = marks[...]
+            for part in range(cap // 128):
+                fbuf[turn - 1, 0, pl.ds(c * (cap // 128) + part, 1), :] = vector[
+                    c : c + 1, part * 128 : part * 128 + 128
+                ]
+
+    def taken(turn, number, c):
+        each = cap // 128
+        return jnp.concatenate(
+            [fbuf[turn - 1, number, pl.ds(c * each + part, 1), :] for part in range(each)], axis=1
+        )
+
+    def direct_copy(number):
+        return pltpu.make_async_remote_copy(
+            src_ref=dbuf.at[0],
+            dst_ref=dbuf.at[number + 1],
+            send_sem=dsend.at[number],
+            recv_sem=drecv.at[number],
+            device_id=device(negated(everyone[number])),
+            device_id_type=MESH_ID,
+        )
+
+    def sum_directly(value):
+        dbuf[0] = value
+        for number in range(len(everyone)):
+            copy = direct_copy(number)
+            copy.start()
+            sent.append(copy)
+        for number in range(len(everyone)):
+            direct_copy(number).wait_recv()
+        return jnp.sum(dbuf[...], axis=0)
+
+    nbuf[0] = marks[...]
     send_round(0)
 
     def build(xi, yi, zi):
         number = slots.index((groups[0][xi][0], groups[1][yi][0], groups[2][zi][0]))
-        info = nbuf[0, number]
+        info = nbuf[number]
         cells = [info[k : k + 1] for k in range(3)]
         fours = [weights(info[k + 3 : k + 4]) for k in range(3)]
         block = (yi * len(groups[2]) + zi) * cap
@@ -215,13 +248,14 @@
         for xi, (off_x, shifts) in enumerate(groups[0]):
             start, planes = span(shifts, size_x)
             rows = planes * rows_y
+            wait_round(turn, off_x)
             for yi, (off_y, _) in enumerate(groups[1]):
                 for zi, (off_z, _) in enumerate(groups[2]):
                     number = slots.index((off_x, off_y, off_z))
                     block = (yi * len(groups[2]) + zi) * cap
                     plane = txy[xi, pl.ds(0, rows), pl.ds(block, cap)]
                     for c in range(3):
-                        high, low = split(plane * nbuf[turn, number, pl.ds(c, 1), :])
+                        high, low = split(plane * taken(turn, number, c))
                         whi[pl.ds(c * rows, rows), pl.ds(block, cap)] = high
                         wlo[pl.ds(c * rows, rows), pl.ds(block, cap)] = low
             high, low = whi[pl.ds(0, 3 * rows), :], wlo[pl.ds(0, 3 * rows), :]
@@ -273,7 +307,6 @@
     target, stiffness, live = aux[pl.ds(0, 3), :], aux[pl.ds(3, 1), :], aux[pl.ds(4, 1), :]
 
     def apply(turn, vector, summing=None):
-        wait_round(turn)
         spread(turn)
         if summing is not None:
             send_sum(summing, 1, wait_sum(summing, 0))
@@ -290,11 +323,9 @@
             for at in range(128, cap, 128):
                 total = total + row[:, at : at + 128]
             folded.append(total)
-        which = lax.broadcasted_iota(jnp.int32, (8, 128), 0)
-        return jnp.where(which == 0, folded[0], jnp.where(which == 1, folded[1], 0.0))
-
-    def totals(turn):
-        tile = wait_sum(turn, 2)
+        return jnp.concatenate(folded, axis=0)
+
+    def totals(tile):
         return (
             jnp.sum(tile[0:1], axis=1, keepdims=True),
             jnp.sum(tile[1:2], axis=1, keepdims=True),
@@ -304,7 +335,8 @@
     residual = live * (target - interpolate(fields[pl.ds(0, 3), pl.ds(1, size_x + 3)]))
     put(1, residual)
     send_round(1)
-    wait_round(0)
+    for off_x, _ in groups[0]:
+        wait_round(0, off_x)
     for xi, yi, zi in itertools.product(*[range(len(group)) for group in groups]):
         if (xi, yi, zi) != (0, 0, 0):
             build(xi, yi, zi)
@@ -314,15 +346,20 @@
     answer = None
     norm_before = alpha = None
     for step in range(ITERS):
-        send_sum(step, 0, partial_sums(residual, image))
+        sums = partial_sums(residual, image)
+        if step + 1 < ITERS or not direct:
+            send_sum(step, 0, sums)
         if step + 1 < ITERS:
             put(step + 2, image)
             send_round(step + 2)
             ahead = apply(step + 2, image, step)
+            norm, product = totals(wait_sum(step, 2))
+        elif direct:
+            norm, product = totals(sum_directly(sums))
         else:
             send_sum(step, 1, wait_sum(step, 0))
             send_sum(step, 2, wait_sum(step, 1))
-        norm, product = totals(step)
+            norm, product = totals(wait_sum(step, 2))
         if step == 0:
             alpha = norm / product
             along_image = ahead
@@ -366,14 +403,18 @@
     tallest = max(span(shifts, size_x)[1] for _, shifts in groups[0])
     longest = max(mesh_counts)
     turns = ITERS + 1
+    devices = mesh_counts[0] * mesh_counts[1] * mesh_counts[2]
+    most = devices if devices <= MOST_DIRECT else 1
     return pl.pallas_call(
         functools.partial(kernel, mesh_counts, sizes),
         out_shape=jax.ShapeDtypeStruct((3, cap), jnp.float32),
         in_specs=[pl.BlockSpec(memory_space=pltpu.VMEM)] * 3,
         out_specs=pl.BlockSpec(memory_space=pltpu.VMEM),
         scratch_shapes=[
-            pltpu.VMEM((turns, number, 8, cap), jnp.float32),
-            pltpu.VMEM((ITERS, 3, longest, 8, 128), jnp.float32),
+            pltpu.VMEM((number, 8, cap), jnp.float32),
+            pltpu.VMEM((ITERS, number, 3 * (cap // 128), 128), jnp.float32),
+            pltpu.VMEM((ITERS, 3, longest, 2, 128), jnp.float32),
+            pltpu.VMEM((most, 2, 128), jnp.float32),
             pltpu.VMEM((len(groups[0]), tallest * rows_y, width), jnp.float32),
             pltpu.VMEM((len(groups[0]), lanes, width), jnp.bfloat16),
             pltpu.VMEM((len(groups[0]), lanes, width), jnp.bfloat16),
@@ -384,6 +425,8 @@
             pltpu.SemaphoreType.DMA((turns, number - 1)),
             pltpu.SemaphoreType.DMA((ITERS, 3, longest - 1)),
             pltpu.SemaphoreType.DMA((ITERS, 3, longest - 1)),
+            pltpu.SemaphoreType.DMA((most,)),
+            pltpu.SemaphoreType.DMA((most,)),
         ],
         compiler_params=pltpu.CompilerParams(
             collective_id=0, has_side_effects=True, vmem_limit_bytes=60 * 1024 * 1024

time: 90.6 us -> 84.8 us (0.936)
  Pallas kernels: 60.4 us -> 54.6 us
    pallas_call x1, Pallas kernels: 60.4 us -> 54.6 us  [body(): pl.pallas_call(functools.partial(kernel, mesh_counts, sizes), out_shape=j...]
  transfers between devices with their start and end apart: 6 -> 6, of which waited for: 5 -> 5; matrix products, arithmetic and copies ran while one was open for 1% -> 2% of each run, Pallas kernels for 0% -> 0%
where the time goes in v2:
time: 84.8 us; the launch traced here: 84.5 us
  Pallas kernels  54.6 us (64%)
  waiting for transfers between devices  14 us (17%)
  starting transfers between devices  8.62 us (10%)
  local copies, waits for them, and re-layouts  3.84 us (5%)
  other arithmetic  2.76 us (3%)
    pallas_call x1, Pallas kernels, body(): pl.pallas_call(functools.partial(kernel, mesh_counts, sizes), out_shape=j...  54.6 us
    ppermute x3, waiting for transfers between devices, extended(): lax.ppermute(tail, axis, [(i, (i + 1) % count) for i in range(count)])  9.66 us
    ppermute x3, starting transfers between devices, extended(): lax.ppermute(head, axis, [((i + 1) % count, i) for i in range(count)])  5.88 us
    ppermute x3, waiting for transfers between devices, extended(): lax.ppermute(head, axis, [((i + 1) % count, i) for i in range(count)])  4.3 us
    ppermute x3, starting transfers between devices, extended(): lax.ppermute(tail, axis, [(i, (i + 1) % count) for i in range(count)])  2.74 us
    unnamed x11, local copies, waits for them, and re-layouts  1.9 us
  transfers between devices with their start and end apart: 6, of which 5 were waited for; matrix products, arithmetic and copies ran while one was open for 2% of the time, Pallas kernels for 0%

profile of v2, /device:TPU:0, one launch (start us, length us, event | category | flops | bytes accessed | tf_op | source)
XLA Modules:
  0.0 84.5 jit_solution(7061960625875110942)
XLA Ops:
  0.0 0.8 rsqrt_bitcast_fusion
  0.8 0.0 copy-start
  0.8 1.0 %slice_maximum_fusion = f32[4,8,8,2]{3,2,1,0:T(8,128)S(1)} fusion(f32[1,8,8,128]{3,2,1,0:T(8,128)S(1)} %rsqrt_bitcast_fusion, f32[3,8,8,128]{3,2,1,0:T(8,128)} %param.8), kind=kLoop, calls=%fused_computation.11 | loop fusion | flops 512 | bytes 133120 | tf_op jit(solution)/shard_map/concatenate | solution.py:395
  1.8 0.5 collective-permute-start
  2.4 0.0 copy-done
  2.4 2.0 %collective-permute-start.1 = (f32[4,8,8,3]{3,2,1,0:T(8,128)S(1)}, f32[4,8,8,3]{3,2,1,0:T(8,128)S(1)}, u32[]{:S(2)}, u32[]{:S(2)}) collective-permute-start(f32[4,8,8,3]{3,2,1,0:T(8,128)S(1)} %pad_maximum_fusion.10), channel_id=1, source_target_pairs={{1,0},{2,1},{3,2},{0,3},{5,4},{6,5},{7,6},{4,7},{9,8},{10,9},{11,1... | collective-permute-start | bytes 9224 | tf_op jit(solution)/shard_map/ppermute | solution.py:31
  4.4 0.0 copy-start.1
  4.4 0.1 pad_add_fusion
  4.5 0.6 copy-done.1
  5.1 0.1 subtract_convert_fusion
  5.8 1.1 %collective-permute-done = f32[4,8,8,2]{3,2,1,0:T(8,128)S(1)} collective-permute-done((f32[4,8,8,2]{3,2,1,0:T(8,128)S(1)}, f32[4,8,8,2]{3,2,1,0:T(8,128)S(1)}, u32[]{:S(2)}, u32[]{:S(2)}) %collective-permute-start) | collective-permute-done | bytes 2080 | tf_op jit(solution)/shard_map/ppermute | solution.py:29
  6.9 1.2 %collective-permute-done.1 = f32[4,8,8,3]{3,2,1,0:T(8,128)S(1)} collective-permute-done((f32[4,8,8,3]{3,2,1,0:T(8,128)S(1)}, f32[4,8,8,3]{3,2,1,0:T(8,128)S(1)}, u32[]{:S(2)}, u32[]{:S(2)}) %collective-permute-start.1) | collective-permute-done | bytes 3104 | tf_op jit(solution)/shard_map/ppermute | solution.py:31
  8.2 0.2 pad_maximum_fusion.7
  8.3 1.6 %collective-permute-start.3 = (f32[4,8,3,133]{3,2,1,0:T(4,128)S(1)}, f32[4,8,3,133]{3,2,1,0:T(4,128)S(1)}, u32[]{:S(2)}, u32[]{:S(2)}) collective-permute-start(f32[4,8,3,133]{3,2,1,0:T(4,128)S(1)} %pad_maximum_fusion.7), channel_id=1, source_target_pairs={{4,0},{0,4},{5,1},{1,5},{6,2},{2,6},{7,3},{3,7},{12,8},{8,12},{13,... | collective-permute-start | bytes 153224 | tf_op jit(solution)/shard_map/ppermute | solution.py:31
  9.9 0.2 pad_maximum_fusion.11
  10.1 0.6 collective-permute-start.2
  10.7 0.1 pad.11.clone
  10.8 0.1 pad.8.clone
  10.8 5.1 %collective-permute-done.2 = f32[4,8,2,133]{3,2,1,0:T(2,128)S(1)} collective-permute-done((f32[4,8,2,133]{3,2,1,0:T(2,128)S(1)}, f32[4,8,2,133]{3,2,1,0:T(2,128)S(1)}, u32[]{:S(2)}, u32[]{:S(2)}) %collective-permute-start.2) | collective-permute-done | bytes 34080 | tf_op jit(solution)/shard_map/ppermute | solution.py:29
  15.9 0.0 collective-permute-done.3
  15.9 0.1 pad_maximum_fusion.6
  16.0 1.6 %collective-permute-start.4 = (f32[4,2,13,133]{3,2,1,0:T(8,128)S(1)}, f32[4,2,13,133]{3,2,1,0:T(8,128)S(1)}, u32[]{:S(2)}, u32[]{:S(2)}) collective-permute-start(f32[4,2,13,133]{3,2,1,0:T(8,128)S(1)} %pad_maximum_fusion.6), channel_id=1, source_target_pairs={{0,8},{8,16},{16,24},{24,0},{1,9},{9,17},{17,25},{25,1},{2,10},{10... | collective-permute-start | bytes 165992 | tf_op jit(solution)/shard_map/ppermute | solution.py:29
  17.7 0.0 copy-start.2
  17.7 0.0 copy-start.3
  17.7 0.1 pad_maximum_fusion.1
  17.8 0.0 copy-start.4
  17.8 2.3 %collective-permute-start.5 = (f32[4,3,13,133]{3,2,1,0:T(8,128)S(1)}, f32[4,3,13,133]{3,2,1,0:T(8,128)S(1)}, u32[]{:S(2)}, u32[]{:S(2)}) collective-permute-start(f32[4,3,13,133]{3,2,1,0:T(8,128)S(1)} %pad_maximum_fusion.1), channel_id=1, source_target_pairs={{8,0},{16,8},{24,16},{0,24},{9,1},{17,9},{25,17},{1,25},{10,2},{18... | collective-permute-start | bytes 248984 | tf_op jit(solution)/shard_map/ppermute | solution.py:31
  20.1 0.0 copy-done.2
  20.1 0.0 copy-done.3
  20.1 0.0 copy-done.4
  20.1 0.7 maximum_maximum_fusion
  20.8 3.5 %collective-permute-done.4 = f32[4,2,13,133]{3,2,1,0:T(8,128)S(1)} collective-permute-done((f32[4,2,13,133]{3,2,1,0:T(8,128)S(1)}, f32[4,2,13,133]{3,2,1,0:T(8,128)S(1)}, u32[]{:S(2)}, u32[]{:S(2)}) %collective-permute-start.4) | collective-permute-done | bytes 55360 | tf_op jit(solution)/shard_map/ppermute | solution.py:29
  24.2 3.1 %collective-permute-done.5 = f32[4,3,13,133]{3,2,1,0:T(8,128)S(1)} collective-permute-done((f32[4,3,13,133]{3,2,1,0:T(8,128)S(1)}, f32[4,3,13,133]{3,2,1,0:T(8,128)S(1)}, u32[]{:S(2)}, u32[]{:S(2)}) %collective-permute-start.5) | collective-permute-done | bytes 83024 | tf_op jit(solution)/shard_map/ppermute | solution.py:31
  27.3 0.3 pad_maximum_fusion
  27.6 1.0 %pad.4.fields = f32[4,13,16,256]{3,2,1,0:T(8,128)} pad(f32[4,13,13,133]{3,2,1,0:T(8,128)S(1)} %pad_maximum_fusion, f32[]{:T(128)} %constant.6.clone.1), padding=0_0x0_0x0_3x0_123 | pad | bytes 1211604 | tf_op jit(solution)/shard_map/jit(_pad)/pad | solution.py:397
  28.6 54.6 %shard_map.73 = f32[3,256]{1,0:T(4,128)} custom-call(f32[4,13,16,256]{3,2,1,0:T(8,128)} %pad.4.fields, f32[8,256]{1,0:T(8,128)} %get-tuple-element.5.marks, f32[8,256]{1,0:T(8,128)} %get-tuple-element.6.aux), custom_call_target="tpu_custom_call" | custom-call | tf_op jit(solution)/shard_map/pallas_call | solution.py:408
  83.2 1.3 %copy.10 = f32[3,256]{1,0:T(4,128)} copy(f32[3,256]{1,0:T(4,128)} %shard_map.73) | data formatting | bytes 6144
  (4 shorter events, 0.0 us)
Async XLA Ops:
  0.8 1.6 %copy-start = (f32[3,8,8,128]{3,2,1,0:T(8,128)S(1)}, f32[3,8,8,128]{3,2,1,0:T(8,128)}, u32[]{:S(2)}) copy-start(f32[3,8,8,128]{3,2,1,0:T(8,128)} %param.8) | copy-start | bytes 294916
  1.8 5.1 %collective-permute-start = (f32[4,8,8,2]{3,2,1,0:T(8,128)S(1)}, f32[4,8,8,2]{3,2,1,0:T(8,128)S(1)}, u32[]{:S(2)}, u32[]{:S(2)}) collective-permute-start(f32[4,8,8,2]{3,2,1,0:T(8,128)S(1)} %slice_maximum_fusion), channel_id=1, source_target_pairs={{0,1},{1,2},{2,3},{3,0},{4,5},{5,6},{6,7},{7,4},{8,9},{9,10},{10,1... | collective-permute-start | bytes 6152 | tf_op jit(solution)/shard_map/ppermute | solution.py:29
  2.4 5.8 %collective-permute-start.1 = (f32[4,8,8,3]{3,2,1,0:T(8,128)S(1)}, f32[4,8,8,3]{3,2,1,0:T(8,128)S(1)}, u32[]{:S(2)}, u32[]{:S(2)}) collective-permute-start(f32[4,8,8,3]{3,2,1,0:T(8,128)S(1)} %pad_maximum_fusion.10), channel_id=1, source_target_pairs={{1,0},{2,1},{3,2},{0,3},{5,4},{6,5},{7,6},{4,7},{9,8},{10,9},{11,1... | collective-permute-start | bytes 9224 | tf_op jit(solution)/shard_map/ppermute | solution.py:31
  4.4 0.7 copy-start.1
  8.3 7.6 %collective-permute-start.3 = (f32[4,8,3,133]{3,2,1,0:T(4,128)S(1)}, f32[4,8,3,133]{3,2,1,0:T(4,128)S(1)}, u32[]{:S(2)}, u32[]{:S(2)}) collective-permute-start(f32[4,8,3,133]{3,2,1,0:T(4,128)S(1)} %pad_maximum_fusion.7), channel_id=1, source_target_pairs={{4,0},{0,4},{5,1},{1,5},{6,2},{2,6},{7,3},{3,7},{12,8},{8,12},{13,... | collective-permute-start | bytes 153224 | tf_op jit(solution)/shard_map/ppermute | solution.py:31
  10.1 5.8 %collective-permute-start.2 = (f32[4,8,2,133]{3,2,1,0:T(2,128)S(1)}, f32[4,8,2,133]{3,2,1,0:T(2,128)S(1)}, u32[]{:S(2)}, u32[]{:S(2)}) collective-permute-start(f32[4,8,2,133]{3,2,1,0:T(2,128)S(1)} %pad_maximum_fusion.11), channel_id=1, source_target_pairs={{0,4},{4,0},{1,5},{5,1},{2,6},{6,2},{3,7},{7,3},{8,12},{12,8},{9,1... | collective-permute-start | bytes 102152 | tf_op jit(solution)/shard_map/ppermute | solution.py:29
  16.0 8.2 %collective-permute-start.4 = (f32[4,2,13,133]{3,2,1,0:T(8,128)S(1)}, f32[4,2,13,133]{3,2,1,0:T(8,128)S(1)}, u32[]{:S(2)}, u32[]{:S(2)}) collective-permute-start(f32[4,2,13,133]{3,2,1,0:T(8,128)S(1)} %pad_maximum_fusion.6), channel_id=1, source_target_pairs={{0,8},{8,16},{16,24},{24,0},{1,9},{9,17},{17,25},{25,1},{2,10},{10... | collective-permute-start | bytes 165992 | tf_op jit(solution)/shard_map/ppermute | solution.py:29
  17.7 2.5 %copy-start.2 = (f32[3,256]{1,0:T(4,128)S(1)}, f32[3,256]{1,0:T(4,128)}, u32[]{:S(2)}) copy-start(f32[3,256]{1,0:T(4,128)} %param.10) | copy-start | bytes 9220
  17.7 2.5 %copy-start.3 = (f32[3,256]{1,0:T(4,128)S(1)}, f32[3,256]{1,0:T(4,128)}, u32[]{:S(2)}) copy-start(f32[3,256]{1,0:T(4,128)} %param.11) | copy-start | bytes 9220
  17.8 2.3 %copy-start.4 = (f32[256]{0:T(256)S(1)}, f32[256]{0:T(256)}, u32[]{:S(2)}) copy-start(f32[256]{0:T(256)} %param.12) | copy-start | bytes 3076
  17.8 9.5 %collective-permute-start.5 = (f32[4,3,13,133]{3,2,1,0:T(8,128)S(1)}, f32[4,3,13,133]{3,2,1,0:T(8,128)S(1)}, u32[]{:S(2)}, u32[]{:S(2)}) collective-permute-start(f32[4,3,13,133]{3,2,1,0:T(8,128)S(1)} %pad_maximum_fusion.1), channel_id=1, source_target_pairs={{8,0},{16,8},{24,16},{0,24},{9,1},{17,9},{25,17},{1,25},{10,2},{18... | collective-permute-start | bytes 248984 | tf_op jit(solution)/shard_map/ppermute | solution.py:31

commit v3 on v2

--- a/solution.py
+++ b/solution.py
@@ -17,22 +17,6 @@
 
 def round_up(value, multiple):
     return -(-value // multiple) * multiple
-
-
-def extended(cells, sides):
-    for axis, dim in sides:
-        count = lax.axis_size(axis)
-        head = lax.slice_in_dim(cells, 0, HIGH, axis=dim)
-        tail = lax.slice_in_dim(cells, cells.shape[dim] - LOW, cells.shape[dim], axis=dim)
-        cells = jnp.concatenate(
-            [
-                lax.ppermute(tail, axis, [(i, (i + 1) % count) for i in range(count)]),
-                cells,
-                lax.ppermute(head, axis, [((i + 1) % count, i) for i in range(count)]),
-            ],
-            axis=dim,
-        )
-    return cells
 
 
 def axis_groups(count):
@@ -84,12 +68,13 @@
 
 
 def kernel(
-    counts, sizes, fields, marks, aux, out, nbuf, fbuf, rbuf, dbuf, txy, thi, tlo, whi, wlo, grid,
-    nsend, nrecv, rsend, rrecv, dsend, drecv,
+    counts, sizes, block, marks, aux, out, fields, xbuf, ybuf, zpack, zbuf, nbuf, fbuf, rbuf, dbuf, txy, thi, tlo, whi, wlo, grid,
+    nsend, nrecv, rsend, rrecv, dsend, drecv, hsend, hrecv,
 ):
     size_x, size_y, size_z = sizes
     cap = marks.shape[1]
     rows_y, lanes = fields.shape[2], fields.shape[3]
+    assert 8 * (size_x + 5) <= size_z == lanes - size_z
     wide_x = size_x + 5
     groups = [axis_groups(count) for count in counts]
     slots = list(itertools.product(*[[offset for offset, _ in group] for group in groups]))
@@ -195,6 +180,78 @@
             direct_copy(number).wait_recv()
         return jnp.sum(dbuf[...], axis=0)
 
+    offs_y = sorted({1 % counts[1], (-1) % counts[1]})
+    offs_z = sorted({1 % counts[2], (-1) % counts[2]})
+
+    def halo_copy(number, source, target, offset):
+        return pltpu.make_async_remote_copy(
+            src_ref=source,
+            dst_ref=target,
+            send_sem=hsend.at[number],
+            recv_sem=hrecv.at[number],
+            device_id=device(negated(offset)),
+            device_id_type=MESH_ID,
+        )
+
+    def go(copies):
+        for copy in copies:
+            copy.start()
+            sent.append(copy)
+
+    low, high = pl.ds(0, LOW), pl.ds(LOW, HIGH)
+    along_x = [
+        halo_copy(0, block.at[:, pl.ds(size_x - LOW, LOW)], xbuf.at[:, low], (counts[0] - 1, 0, 0)),
+        halo_copy(1, block.at[:, pl.ds(0, HIGH)], xbuf.at[:, high], (1, 0, 0)),
+    ]
+    along_y, relayed_y = [], []
+    for k, off in enumerate(offs_y):
+        here = (0, off, 0)
+        along_y.append(halo_copy(2 + k, block, ybuf.at[k, :, pl.ds(LOW, size_x)], here))
+        relayed_y.append(halo_copy(4 + k, xbuf.at[:, low], ybuf.at[k, :, low], here))
+        relayed_y.append(
+            halo_copy(6 + k, xbuf.at[:, high], ybuf.at[k, :, pl.ds(LOW + size_x, HIGH)], here)
+        )
+    along_z = [halo_copy(8 + k, zpack, zbuf.at[k], (0, 0, off)) for k, off in enumerate(offs_z)]
+
+    def widen():
+        for copy in along_y + relayed_y:
+            copy.wait_recv()
+        below = ybuf.at[offs_y.index((-1) % counts[1])]
+        above = ybuf.at[offs_y.index(1 % counts[1])]
+        lane = lax.broadcasted_iota(jnp.int32, (4, rows_y, size_z), 2)
+        zero = jnp.zeros((4, rows_y - size_y - LOW - HIGH, size_z), jnp.float32)
+        packed = jnp.zeros((4, rows_y, size_z), jnp.float32)
+        for plane in range(wide_x):
+            if plane < LOW:
+                own = xbuf[:, plane]
+            elif plane < LOW + size_x:
+                own = block[:, plane - LOW]
+            else:
+                own = xbuf[:, plane - size_x]
+            tall = jnp.concatenate(
+                [below[:, plane][:, size_y - LOW :], own, above[:, plane][:, :HIGH], zero], axis=1
+            )
+            fields[:, plane, :, pl.ds(0, size_z)] = tall
+            ends = jnp.where(lane < HIGH, tall, pltpu.roll(tall, LOW + HIGH, 2))
+            at = 8 * plane
+            inside = (lane >= at) & (lane < at + LOW + HIGH)
+            packed = jnp.where(inside, pltpu.roll(ends, at, 2) if at else ends, packed)
+        zpack[...] = packed
+        go(along_z)
+        for copy in along_z:
+            copy.wait_recv()
+        before = zbuf[offs_z.index((-1) % counts[2])]
+        after = zbuf[offs_z.index(1 % counts[2])]
+        for plane in range(wide_x):
+            at = 8 * plane
+            tall = pltpu.roll(fields[:, plane, :, pl.ds(0, size_z)], LOW, 2)
+            first = pltpu.roll(before, (-(at + HIGH)) % size_z, 2)
+            last = pltpu.roll(after, (LOW - at) % size_z, 2)
+            fields[:, plane, :, pl.ds(0, size_z)] = jnp.where(lane < LOW, first, tall)
+            tail = jnp.where(lane < LOW, tall, jnp.where(lane < LOW + HIGH, last, 0.0))
+            fields[:, plane, :, pl.ds(size_z, lanes - size_z)] = tail
+
+    go(along_x + along_y)
     nbuf[0] = marks[...]
     send_round(0)
 
@@ -332,14 +389,18 @@
         )
 
     build(0, 0, 0)
-    residual = live * (target - interpolate(fields[pl.ds(0, 3), pl.ds(1, size_x + 3)]))
-    put(1, residual)
-    send_round(1)
+    for copy in along_x:
+        copy.wait_recv()
+    go(relayed_y)
     for off_x, _ in groups[0]:
         wait_round(0, off_x)
     for xi, yi, zi in itertools.product(*[range(len(group)) for group in groups]):
         if (xi, yi, zi) != (0, 0, 0):
             build(xi, yi, zi)
+    widen()
+    residual = live * (target - interpolate(fields[pl.ds(0, 3), pl.ds(1, size_x + 3)]))
+    put(1, residual)
+    send_round(1)
 
     image = apply(1, residual)
     direction, along, along_image = residual, image, None
@@ -393,10 +454,6 @@
         [target, stiffness[None], live[None], jnp.zeros((3, cap), jnp.float32)], axis=0
     )
     stacked = jnp.concatenate([base_velocity, lax.rsqrt(density)[None]], axis=0)
-    fields = extended(stacked, (("gz", 3), ("gy", 2), ("gx", 1)))
-    fields = jnp.pad(
-        fields, ((0, 0), (0, 0), (0, rows_y - size_y - 5), (0, lanes - size_z - 5))
-    )
     groups = [axis_groups(count) for count in mesh_counts]
     number = len(groups[0]) * len(groups[1]) * len(groups[2])
     width = len(groups[1]) * len(groups[2]) * cap
@@ -411,6 +468,11 @@
         in_specs=[pl.BlockSpec(memory_space=pltpu.VMEM)] * 3,
         out_specs=pl.BlockSpec(memory_space=pltpu.VMEM),
         scratch_shapes=[
+            pltpu.VMEM((4, size_x + 5, rows_y, lanes), jnp.float32),
+            pltpu.VMEM((4, LOW + HIGH, size_y, size_z), jnp.float32),
+            pltpu.VMEM((2, 4, size_x + 5, size_y, size_z), jnp.float32),
+            pltpu.VMEM((4, rows_y, size_z), jnp.float32),
+            pltpu.VMEM((2, 4, rows_y, size_z), jnp.float32),
             pltpu.VMEM((number, 8, cap), jnp.float32),
             pltpu.VMEM((ITERS, number, 3 * (cap // 128), 128), jnp.float32),
             pltpu.VMEM((ITERS, 3, longest, 2, 128), jnp.float32),
@@ -427,11 +489,13 @@
             pltpu.SemaphoreType.DMA((ITERS, 3, longest - 1)),
             pltpu.SemaphoreType.DMA((most,)),
             pltpu.SemaphoreType.DMA((most,)),
+            pltpu.SemaphoreType.DMA((10,)),
+            pltpu.SemaphoreType.DMA((10,)),
         ],
         compiler_params=pltpu.CompilerParams(
             collective_id=0, has_side_effects=True, vmem_limit_bytes=60 * 1024 * 1024
         ),
-    )(fields, marks, aux)
+    )(stacked, marks, aux)
 
 
 def solution(mesh):

time: 84.8 us -> 73.6 us (0.87)
  waiting for transfers between devices: 14 us -> 0 us
  Pallas kernels: 54.6 us -> 66.7 us
  starting transfers between devices: 8.62 us -> 0 us
    ppermute x6 -> x0, waiting for transfers between devices: 14 us -> none  [the longest x3 9.66 us: extended(): lax.ppermute(tail, axis, [(i, (i + 1) % count) for i in range(count)])]
    pallas_call x1, Pallas kernels: 54.6 us -> 66.7 us  [body(): pl.pallas_call(functools.partial(kernel, mesh_counts, sizes), out_shape=j...]
    ppermute x6 -> x0, starting transfers between devices: 8.62 us -> none  [the longest x3 5.88 us: extended(): lax.ppermute(head, axis, [((i + 1) % count, i) for i in range(count)])]
    pad x1 -> x0, local copies, waits for them, and re-layouts: 1.02 us -> none  [body(): jnp.pad(fields, ((0, 0), (0, 0), (0, rows_y - size_y - 5), (0, lanes - si...]
    unnamed x11 -> x9, local copies, waits for them, and re-layouts: 1.9 us -> 2.55 us
  transfers between devices with their start and end apart: 6 -> 0, of which waited for: 5 -> 0; matrix products, arithmetic and copies ran while one was open for 2% -> 0% of each run, Pallas kernels for 0% -> 0%
where the time goes in v3:
time: 73.6 us; the launch traced here: 73.3 us
  Pallas kernels  66.7 us (91%)
  local copies, waits for them, and re-layouts  3.47 us (5%)
  other arithmetic  2.38 us (3%)
    pallas_call x1, Pallas kernels, body(): pl.pallas_call(functools.partial(kernel, mesh_counts, sizes), out_shape=j...  66.7 us
    unnamed x9, local copies, waits for them, and re-layouts  2.55 us
    concatenate x1, other arithmetic, body(): stacked = jnp.concatenate([base_velocity, lax.rsqrt(density)[None]], axis=0)  1.56 us

profile of v3, /device:TPU:0, one launch (start us, length us, event | category | flops | bytes accessed | tf_op | source)
XLA Modules:
  0.0 73.3 jit_solution(2110244708088033304)
XLA Ops:
  0.0 0.8 %rsqrt_bitcast_fusion = f32[1,8,8,128]{3,2,1,0:T(8,128)S(1)} fusion(f32[8,8,128]{2,1,0:T(8,128)} %param.7), kind=kLoop, calls=%fused_computation.1 | loop fusion | bytes 65536 | tf_op jit(solution)/shard_map/broadcast_in_dim | solution.py:456
  0.8 1.6 %pad_maximum_fusion.block = f32[4,8,8,128]{3,2,1,0:T(8,128)} fusion(f32[1,8,8,128]{3,2,1,0:T(8,128)S(1)} %rsqrt_bitcast_fusion, f32[3,8,8,128]{3,2,1,0:T(8,128)} %param.8), kind=kLoop, calls=%fused_computation | loop fusion | flops 32768 | bytes 262144 | tf_op jit(solution)/shard_map/concatenate | solution.py:456
  2.3 0.0 copy-start
  2.3 0.1 pad_add_fusion
  2.4 0.6 copy-done
  3.0 0.1 subtract_convert_fusion
  3.1 0.1 pad.6.clone
  3.2 0.0 copy-start.2
  3.2 0.1 pad.3.clone
  3.2 0.0 copy-start.1
  3.9 0.0 copy-start.3
  3.9 0.0 copy-done.2
  3.9 0.0 copy-done.1
  4.0 0.7 copy-done.3
  4.6 0.7 maximum_maximum_fusion
  5.3 66.7 %shard_map.73 = f32[3,256]{1,0:T(4,128)} custom-call(f32[4,8,8,128]{3,2,1,0:T(8,128)} %pad_maximum_fusion.block, f32[8,256]{1,0:T(8,128)} %get-tuple-element.5.marks, f32[8,256]{1,0:T(8,128)} %get-tuple-element.6.aux), custom_call_target="tpu_custom_call" | custom-call | tf_op jit(solution)/shard_map/pallas_call | solution.py:465
  72.0 1.3 %copy.10 = f32[3,256]{1,0:T(4,128)} copy(f32[3,256]{1,0:T(4,128)} %shard_map.73) | data formatting | bytes 6144
  (3 shorter events, 0.0 us)
Async XLA Ops:
  2.3 0.7 copy-start
  3.2 0.8 %copy-start.2 = (f32[3,256]{1,0:T(4,128)S(1)}, f32[3,256]{1,0:T(4,128)}, u32[]{:S(2)}) copy-start(f32[3,256]{1,0:T(4,128)} %param.11) | copy-start | bytes 9220
  3.2 0.7 copy-start.1
  3.9 0.7 copy-start.3

commit v4 on v3

--- a/solution.py
+++ b/solution.py
@@ -305,10 +305,11 @@
         for xi, (off_x, shifts) in enumerate(groups[0]):
             start, planes = span(shifts, size_x)
             rows = planes * rows_y
-            wait_round(turn, off_x)
             for yi, (off_y, _) in enumerate(groups[1]):
                 for zi, (off_z, _) in enumerate(groups[2]):
                     number = slots.index((off_x, off_y, off_z))
+                    if number:
+                        neighbour_copy(turn, number).wait_recv()
                     block = (yi * len(groups[2]) + zi) * cap
                     plane = txy[xi, pl.ds(0, rows), pl.ds(block, cap)]
                     for c in range(3):

time: 73.6 us -> 75.1 us (1.020)
  Pallas kernels: 66.7 us -> 68.2 us
    pallas_call x1, Pallas kernels: 66.7 us -> 68.2 us  [body(): pl.pallas_call(functools.partial(kernel, mesh_counts, sizes), out_shape=j...]
where the time goes in v4:
time: 75.1 us; the launch traced here: 74.8 us
  Pallas kernels  68.2 us (91%)
  local copies, waits for them, and re-layouts  3.47 us (5%)
  other arithmetic  2.38 us (3%)
    pallas_call x1, Pallas kernels, body(): pl.pallas_call(functools.partial(kernel, mesh_counts, sizes), out_shape=j...  68.2 us
    unnamed x9, local copies, waits for them, and re-layouts  2.55 us
    concatenate x1, other arithmetic, body(): stacked = jnp.concatenate([base_velocity, lax.rsqrt(density)[None]], axis=0)  1.56 us

profile of v4, /device:TPU:0, one launch (start us, length us, event | category | flops | bytes accessed | tf_op | source)
XLA Modules:
  0.0 74.8 jit_solution(11121105604111806737)
XLA Ops:
  0.0 0.8 %rsqrt_bitcast_fusion = f32[1,8,8,128]{3,2,1,0:T(8,128)S(1)} fusion(f32[8,8,128]{2,1,0:T(8,128)} %param.7), kind=kLoop, calls=%fused_computation.1 | loop fusion | bytes 65536 | tf_op jit(solution)/shard_map/broadcast_in_dim | solution.py:457
  0.8 1.6 %pad_maximum_fusion.block = f32[4,8,8,128]{3,2,1,0:T(8,128)} fusion(f32[1,8,8,128]{3,2,1,0:T(8,128)S(1)} %rsqrt_bitcast_fusion, f32[3,8,8,128]{3,2,1,0:T(8,128)} %param.8), kind=kLoop, calls=%fused_computation | loop fusion | flops 32768 | bytes 262144 | tf_op jit(solution)/shard_map/concatenate | solution.py:457
  2.3 0.0 copy-start
  2.3 0.1 pad_add_fusion
  2.4 0.6 copy-done
  3.0 0.1 subtract_convert_fusion
  3.1 0.1 pad.6.clone
  3.2 0.0 copy-start.2
  3.2 0.1 pad.3.clone
  3.2 0.0 copy-start.1
  3.9 0.0 copy-start.3
  3.9 0.0 copy-done.2
  3.9 0.0 copy-done.1
  4.0 0.7 copy-done.3
  4.6 0.7 maximum_maximum_fusion
  5.3 68.2 %shard_map.73 = f32[3,256]{1,0:T(4,128)} custom-call(f32[4,8,8,128]{3,2,1,0:T(8,128)} %pad_maximum_fusion.block, f32[8,256]{1,0:T(8,128)} %get-tuple-element.5.marks, f32[8,256]{1,0:T(8,128)} %get-tuple-element.6.aux), custom_call_target="tpu_custom_call" | custom-call | tf_op jit(solution)/shard_map/pallas_call | solution.py:466
  73.5 1.3 %copy.10 = f32[3,256]{1,0:T(4,128)} copy(f32[3,256]{1,0:T(4,128)} %shard_map.73) | data formatting | bytes 6144
  (3 shorter events, 0.0 us)
Async XLA Ops:
  2.3 0.7 copy-start
  3.2 0.8 %copy-start.2 = (f32[3,256]{1,0:T(4,128)S(1)}, f32[3,256]{1,0:T(4,128)}, u32[]{:S(2)}) copy-start(f32[3,256]{1,0:T(4,128)} %param.11) | copy-start | bytes 9220
  3.2 0.7 copy-start.1
  3.9 0.7 copy-start.3
